TPU v7x, 32 devices: a whole 2x2x4 slice. The times are simulated.
32 devices in a mesh: groups: 2 (over x), ctx: 8 (over z, y), tp: 2 (over core).
Axes of the slice: x: 2, y: 2, z: 4, core: 2. Of those that a mesh axis runs over, the one named last changes fastest.
Arguments:
- tokens: bfloat16 [8192, 2048], P(('groups', 'ctx')), parts along dimension 0, may hold values from -6 to 6
- weight: bfloat16 [2048, 3, 2048], P('ctx', None, 'tp'), may hold values from -0.125 to 0.125
- adapter_a: bfloat16 [2048, 16], replicated, may hold values from -2.390625 to 2.390625
- adapter_b: bfloat16 [16, 3, 2048], P(None, None, 'tp'), may hold values from -2.390625 to 2.390625
- short_filter: float32 [7, 3, 2048], P(None, None, 'tp'), may hold values from -1.8 to 1.8
- long_filter: float32 [128, 2048], P(None, 'tp'), may hold values from -0.54 to 0.54
- skip_gain: float32 [2048], P('tp'), may hold values from -4.2 to 4.2
- cotangent: bfloat16 [8192, 2048], P(('groups', 'ctx'), 'tp'), parts along dimension 0, may hold values from -6 to 6
Outputs:
- mixed: bfloat16 [8192, 2048], P(('groups', 'ctx'), 'tp'), parts along dimension 0
- grad_tokens: bfloat16 [8192, 2048], P(('groups', 'ctx'), 'tp'), parts along dimension 0
- grad_a: float32 [4096, 16], P('groups'), parts along dimension 0
- grad_b: float32 [32, 3, 2048], P('groups', None, 'tp'), parts along dimension 0
There are 2 independent parts, one for each index of `groups`. A program takes and returns all parts, laid end to end along the dimension named above; an argument that names none is the same for every part. Nothing has to cross between parts.
All inputs are finite; a program needn't handle non-finite values.
Results may differ from a plain program's by a relative error of at most 0.0093.
Values may be sent and summed in bfloat16 or wider, within the bound.
A program may use at most 128 MiB of HBM per device.

v0:
```python
import math

import jax
import jax.numpy as jnp
from jax import lax
from jax.sharding import PartitionSpec as P

adapter_scale = 0.03125


def shifted(value, axis, steps):
    count = lax.axis_size(axis)
    initial, last = (max(0, -steps), min(count, count - steps))
    return lax.ppermute(value, axis, [(source, source + steps) for source in range(initial, last)])


def causal(signal, filter_taps):
    return lax.conv_general_dilated(
        signal[None],
        filter_taps[::-1][:, None, :],
        (1,),
        "VALID",
        dimension_numbers=("NWC", "WIO", "NWC"),
        feature_group_count=signal.shape[1],
        precision=lax.Precision.HIGHEST,
    )[0]


def anticausal(signal, filter_taps):
    return lax.conv_general_dilated(
        signal[None],
        filter_taps[:, None, :],
        (1,),
        "VALID",
        dimension_numbers=("NWC", "WIO", "NWC"),
        feature_group_count=signal.shape[1],
        precision=lax.Precision.HIGHEST,
    )[0]


def body(tokens, weight, adapter_a, adapter_b, short_filter, long_filter, skip_gain, cotangent):
    row_count = tokens.shape[0]
    share_rows = weight.shape[0]
    channels = weight.shape[2]
    adapter_rank = adapter_a.shape[1]
    short_taps = short_filter.shape[0]
    long_taps = long_filter.shape[0]
    seq_total = row_count * lax.axis_size("ctx")
    first_row = lax.axis_index("ctx") * share_rows
    own_rows = lax.dynamic_slice_in_dim(adapter_a, first_row, share_rows, 0)
    flat_b = adapter_b.reshape(adapter_rank, 3 * channels)
    delta_w = jnp.dot(own_rows, flat_b, preferred_element_type=jnp.float32)
    merged = (
        weight.reshape(share_rows, 3 * channels).astype(jnp.float32) + adapter_scale * delta_w
    ).astype(jnp.bfloat16)
    packed = jnp.dot(
        tokens,
        lax.all_gather(merged, "ctx", axis=0, tiled=True),
        preferred_element_type=jnp.float32,
    ).astype(jnp.bfloat16)
    short_flat = short_filter.reshape(short_taps, 3 * channels)
    earlier = shifted(packed[row_count - (short_taps - 1) :], "ctx", 1)
    short_out = causal(jnp.concatenate([earlier, packed], axis=0).astype(jnp.float32), short_flat)
    query = short_out[:, :channels]
    keyed = short_out[:, channels : 2 * channels]
    valued = short_out[:, 2 * channels :]
    gated = (keyed * valued).astype(jnp.bfloat16)
    earlier_gated = shifted(gated[row_count - (long_taps - 1) :], "ctx", 1)
    gated_pad = jnp.concatenate([earlier_gated, gated], axis=0)
    filtered = causal(gated_pad.astype(jnp.float32), long_filter) + skip_gain * gated.astype(
        jnp.float32
    )
    mixed = (query * filtered).astype(jnp.bfloat16)
    cot_f = cotangent.astype(jnp.float32)
    grad_filtered = (cot_f * query).astype(jnp.bfloat16)
    later = shifted(grad_filtered[: long_taps - 1], "ctx", -1)
    grad_gated = anticausal(
        jnp.concatenate([grad_filtered, later], axis=0).astype(jnp.float32), long_filter
    ) + skip_gain * grad_filtered.astype(jnp.float32)
    grad_short = jnp.concatenate(
        [cot_f * filtered, grad_gated * valued, grad_gated * keyed], axis=1
    ).astype(jnp.bfloat16)
    later_short = shifted(grad_short[: short_taps - 1], "ctx", -1)
    grad_packed = anticausal(
        jnp.concatenate([grad_short, later_short], axis=0).astype(jnp.float32), short_flat
    ).astype(jnp.bfloat16)
    partial_grad = lax.dot_general(
        grad_packed,
        lax.all_gather(merged, "ctx", axis=0, tiled=True),
        (((1,), (1,)), ((), ())),
        preferred_element_type=jnp.float32,
    )
    grad_tokens = lax.psum_scatter(
        partial_grad.astype(jnp.bfloat16), "tp", scatter_dimension=1, tiled=True
    )
    projected = jnp.dot(tokens, adapter_a, preferred_element_type=jnp.float32).astype(jnp.bfloat16)
    part_b = lax.dot_general(
        projected, grad_packed, (((0,), (0,)), ((), ())), preferred_element_type=jnp.float32
    )
    local_through = lax.dot_general(
        grad_packed, flat_b, (((1,), (1,)), ((), ())), preferred_element_type=jnp.float32
    )
    through_b = lax.psum(local_through, "tp").astype(jnp.bfloat16)
    part_a = lax.dot_general(
        tokens, through_b, (((0,), (0,)), ((), ())), preferred_element_type=jnp.float32
    )
    sum_a, sum_b = lax.psum((part_a, part_b), "ctx")
    factor = adapter_scale / math.sqrt(seq_total)
    return (mixed, grad_tokens, sum_a * factor, (sum_b * factor).reshape(adapter_rank, 3, channels))


def solution(mesh):
    return jax.shard_map(
        body,
        mesh=mesh,
        in_specs=(
            P(("groups", "ctx"), None),
            P("ctx", None, "tp"),
            P(),
            P(None, None, "tp"),
            P(None, None, "tp"),
            P(None, "tp"),
            P("tp"),
            P(("groups", "ctx"), "tp"),
        ),
        out_specs=(
            P(("groups", "ctx"), "tp"),
            P(("groups", "ctx"), "tp"),
            P("groups", None),
            P("groups", None, "tp"),
        ),
        check_vma=False,
    )
```

profile of v0, /device:TPU:24, one launch (start us, length us, event | category | flops | bytes accessed | tf_op | source)
XLA Modules:
  0.0 449.2 jit_solution(4179814984877696524)
XLA Ops:
  8.3 2.6 copy.21
  10.9 3.3 bitcast_convert_fusion
  14.2 3.6 copy.23
  17.8 3.7 fusion.4
  21.5 175.6 %all-gather.2.cloned.1.call-done = bf16[2048,3072]{1,0:T(8,128)(2,1)} async-done(((bf16[256,3072]{1,0:T(8,128)(2,1)}), bf16[2048,3072]{1,0:T(8,128)(2,1)}) %all-gather.2.cloned.1.call-update) | async-done | bytes 12582928 | tf_op jit(solution)/shard_map/all_gather | solution.py:58
  197.1 9.6 %fusion.2 = bf16[512,3072]{1,0:T(8,128)(2,1)S(1)} fusion(bf16[512,2048]{1,0:T(8,128)(2,1)S(1)} %copy-done, bf16[2048,3072]{1,0:T(8,128)(2,1)} %all-gather.2.cloned.1.call-done), kind=kOutput, calls=%fused_computation.7 | convolution fusion | flops 6444023808 | bytes 17825792 | tf_op jit(solution)/shard_map/dot_general | solution.py:56
  211.6 3.7 collective-permute-done
  215.3 2.7 maximum_bitcast_fusion
  219.9 4.6 %reshape.28 = bf16[1,8,65,3072]{3,2,1,0:T(8,128)(2,1)} reshape(bf16[1,520,3072]{2,1,0:T(8,128)(2,1)} %pad) | data formatting | bytes 6389760 | tf_op jit(solution)/shard_map/conv_general_dilated | solution.py:18
  224.5 3.8 copy.25
  228.4 3.3 convolution_select_fusion
  231.8 6.5 %copy.26 = f32[8,65,3072]{2,1,0:T(8,128)} copy(f32[8,65,3072]{2,0,1:T(8,128)S(1)} %convolution_select_fusion) | data formatting | bytes 12779520 | tf_op jit(solution)/shard_map/conv_general_dilated | solution.py:18
  238.3 6.7 %reshape.32 = f32[1,520,3072]{2,1,0:T(8,128)} reshape(f32[8,65,3072]{2,1,0:T(8,128)} %copy.26) | data formatting | bytes 12779520 | tf_op jit(solution)/shard_map/conv_general_dilated | solution.py:18
  245.0 3.3 slice_bitcast_fusion
  252.0 2.6 collective-permute-start.2
  254.6 4.7 %rev.7 = f32[128,1024]{1,0:T(8,128)} reverse(f32[128,1024]{1,0:T(8,128)} %param.13), dimensions={0} | reverse | bytes 1048576 | tf_op jit(solution)/shard_map/rev | solution.py:20
  260.4 3.3 collective-permute-start.1
  263.9 22.5 %fusion.17 = f32[1,512,1024]{2,0,1:T(1,128)S(1)} fusion(bf16[1,639,1024]{2,1,0:T(8,128)(2,1)S(1)} %maximum_bitcast_fusion.3, f32[128,1,1024]{2,0,1:T(8,128)S(1)} %bitcast.63), kind=kOutput, calls=%fused_computation.27 | convolution fusion | flops 805306368 | bytes 3930112 | tf_op jit(solution)/shard_map/conv_general_dilated | solution.py:30
  286.8 22.5 %fusion.19 = f32[1,512,1024]{2,0,1:T(1,128)S(1)} fusion(bf16[1,639,1024]{2,1,0:T(8,128)(2,1)S(1)} %maximum_bitcast_fusion.2, f32[128,1,1024]{2,0,1:T(8,128)S(1)} %bitcast.64), kind=kOutput, calls=%fused_computation.29 | convolution fusion | flops 805306368 | bytes 3930112 | tf_op jit(solution)/shard_map/conv_general_dilated | solution.py:18
  309.3 3.3 multiply_convert_fusion.1
  312.7 3.5 collective-permute-start.3
  322.7 4.6 %reshape.35 = bf16[1,8,65,3072]{3,2,1,0:T(8,128)(2,1)} reshape(bf16[1,520,3072]{2,1,0:T(8,128)(2,1)} %pad.2) | data formatting | bytes 6389760 | tf_op jit(solution)/shard_map/conv_general_dilated | solution.py:30
  327.3 3.8 copy.32
  331.2 6.1 %select_convert_fusion = bf16[8,65,3072]{2,0,1:T(8,128)(2,1)S(1)} fusion(bf16[1,7,6,3072]{3,1,2,0:T(8,128)(2,1)S(1)} %slice.40, bf16[1,8,65,3072]{3,1,2,0:T(8,128)(2,1)S(1)} %copy.32, pred[8,65]{0,1:T(8,128)(4,1)S(1)} %copy-done.13, f32[7,1,3072]{2,0,1:T(8,128)S(1)} %bitcast.70), kind=kOutput, calls=%fused_computation.3 | convolution fusion | flops 147849216 | bytes 6734344 | tf_op jit(solution)/shard_map/conv_general_dilated | solution.py:30
  337.3 3.5 copy.34
  340.8 4.7 %reshape.39 = bf16[1,520,3072]{2,1,0:T(8,128)(2,1)} reshape(bf16[8,65,3072]{2,1,0:T(8,128)(2,1)} %copy.34) | data formatting | bytes 6389760 | tf_op jit(solution)/shard_map/convert_element_type | solution.py:86
  345.5 2.9 fusion.22
  348.4 4.5 %fusion.21 = f32[16,3072]{1,0:T(8,128)} fusion(bf16[1,520,3072]{2,1,0:T(8,128)(2,1)} %reshape.39, bf16[512,2048]{1,0:T(8,128)(2,1)S(1)} %copy-done, bf16[2048,16]{0,1:T(8,128)(2,1)S(1)} %copy-done.11), kind=kOutput, calls=%fused_computation.31 | convolution fusion | flops 83894272 | bytes 5505024 | tf_op jit(solution)/shard_map/dot_general | solution.py:97
  352.9 4.2 psum.21
  358.2 11.8 %convolution_convert_fusion.1 = bf16[512,2048]{1,0:T(8,128)(2,1)} fusion(bf16[2048,3072]{1,0:T(8,128)(2,1)} %all-gather.2.cloned.1.call-done, bf16[1,520,3072]{2,1,0:T(8,128)(2,1)} %reshape.39), kind=kOutput, calls=%fused_computation.24 | convolution fusion | flops 6443499520 | bytes 17825792 | tf_op jit(solution)/shard_map/dot_general | solution.py:87
  370.0 59.5 %all-reduce.3.cloned.1.call-done = (f32[2048,16]{0,1:T(8,128)}, f32[16,3072]{1,0:T(8,128)}) async-done(((f32[2048,16]{0,1:T(8,128)}, f32[16,3072]{1,0:T(8,128)}), (f32[2048,16]{0,1:T(8,128)}, f32[16,3072]{1,0:T(8,128)})) %all-reduce.3.cloned.1.call-update) | async-done | bytes 327696 | tf_op jit(solution)/shard_map/psum | solution.py:107
  432.7 9.8 %reduce-scatter.2.cloned.1.call-done = bf16[512,1024]{1,0:T(8,128)(2,1)} async-done(((bf16[512,2048]{1,0:T(8,128)(2,1)}), bf16[512,1024]{1,0:T(8,128)(2,1)}) %reduce-scatter.2.cloned.1.call-update) | async-done | bytes 1048592 | tf_op jit(solution)/shard_map/reduce_scatter | solution.py:93
  (62 shorter events, 24.2 us)
Async XLA Ops:
  7.2 189.9 %copy-start = (bf16[512,2048]{1,0:T(8,128)(2,1)S(1)}, bf16[512,2048]{1,0:T(8,128)(2,1)}, u32[]{:S(2)}) copy-start(bf16[512,2048]{1,0:T(8,128)(2,1)} %param.8) | copy-start | bytes 6291460
  7.2 189.9 %all-gather.2.cloned.1.call-start = ((), (), s32[]{:S(2)}) async-start(), calls=%async_computation.1 | async-start | bytes 14155776 | tf_op jit(solution)/shard_map/all_gather | solution.py:58
  8.3 9.5 %copy-start.8 = (bf16[3,2,8,1024]{3,2,0,1:T(8,128)(2,1)}, bf16[3,2,8,1024]{3,2,0,1:T(8,128)(2,1)S(1)}, u32[]{:S(2)}) copy-start(bf16[3,2,8,1024]{3,2,0,1:T(8,128)(2,1)S(1)} %copy.39) | copy-start | bytes 294916
  21.4 189.3 %copy-start.10 = (f32[7,3,1024]{2,0,1:T(8,128)S(1)}, f32[7,3,1024]{2,0,1:T(8,128)}, u32[]{:S(2)}) copy-start(f32[7,3,1024]{2,0,1:T(8,128)} %param.12) | copy-start | bytes 258052
  21.5 408.1 %all-reduce.3.cloned.1.call-start = ((), (), s32[]{:S(2)}) async-start(), calls=%async_computation.3 | async-start | bytes 655360 | tf_op jit(solution)/shard_map/psum | solution.py:107
  206.7 1.7 copy-start.5
  208.4 6.9 %collective-permute-start = (bf16[6,3072]{1,0:T(8,128)(2,1)S(1)}, bf16[6,3072]{1,0:T(8,128)(2,1)S(1)}, u32[]{:S(2)}, u32[]{:S(2)}) collective-permute-start(bf16[6,3072]{1,0:T(8,128)(2,1)S(1)} %slice.32), channel_id=1, source_target_pairs={{0,2},{2,4},{4,6},{6,8},{8,10},{10,12},{12,14},{1,3},{3,5},{5,7},{... | collective-permute-start | bytes 110600 | tf_op jit(solution)/shard_map/ppermute | solution.py:14
  224.5 3.9 copy-start.13
  245.0 3.3 copy-start.3
  248.3 3.0 copy-start.1
  252.0 11.7 %collective-permute-start.2 = (bf16[127,1024]{1,0:T(8,128)(2,1)}, bf16[127,1024]{1,0:T(8,128)(2,1)S(1)}, u32[]{:S(2)}, u32[]{:S(2)}) collective-permute-start(bf16[127,1024]{1,0:T(8,128)(2,1)} %slice.39), channel_id=1, source_target_pairs={{2,0},{4,2},{6,4},{8,6},{10,8},{12,10},{14,12},{3,1},{5,3},{7,5},{... | collective-permute-start | bytes 780296 | tf_op jit(solution)/shard_map/ppermute | solution.py:14
  259.3 4.5 copy-start.6
  260.4 26.0 %collective-permute-start.1 = (bf16[127,1024]{1,0:T(8,128)(2,1)S(1)}, bf16[127,1024]{1,0:T(8,128)(2,1)S(1)}, u32[]{:S(2)}, u32[]{:S(2)}) collective-permute-start(bf16[127,1024]{1,0:T(8,128)(2,1)S(1)} %slice.38), channel_id=1, source_target_pairs={{0,2},{2,4},{4,6},{6,8},{8,10},{10,12},{12,14},{1,3},{3,5},{5,7},{... | collective-permute-start | bytes 780296 | tf_op jit(solution)/shard_map/ppermute | solution.py:14
  263.8 22.6 %copy-start.2 = (bf16[512,1024]{1,0:T(8,128)(2,1)S(1)}, bf16[512,1024]{1,0:T(8,128)(2,1)}, u32[]{:S(2)}) copy-start(bf16[512,1024]{1,0:T(8,128)(2,1)} %get-tuple-element.18) | copy-start | bytes 3145732
  263.9 22.9 %copy-start.7 = (f32[128,1024]{1,0:T(8,128)S(1)}, f32[128,1024]{1,0:T(8,128)}, u32[]{:S(2)}) copy-start(f32[128,1024]{1,0:T(8,128)} %rev.7) | copy-start | bytes 1572868
  263.9 45.4 %slice-start = ((s8[6291456]{0:T(1024)(128)(4,1)}), s8[4194304]{0:T(1024)(128)(4,1)S(1)}, s32[]{:S(2)}) async-start(s8[6291456]{0:T(1024)(128)(4,1)} %bitcast.60), calls=%async_computation.4 | async-start | bytes 8388608
  286.4 22.9 %slice-start.1 = ((s8[6291456]{0:T(1024)(128)(4,1)}), s8[2097152]{0:T(1024)(128)(4,1)S(1)}, s32[]{:S(2)}) async-start(s8[6291456]{0:T(1024)(128)(4,1)} %bitcast.60), calls=%async_computation.5 | async-start | bytes 4194304
  286.7 22.6 %copy-start.4 = (bf16[512,1024]{1,0:T(8,128)(2,1)S(1)}, bf16[512,1024]{1,0:T(8,128)(2,1)}, u32[]{:S(2)}) copy-start(bf16[512,1024]{1,0:T(8,128)(2,1)} %param.15) | copy-start | bytes 3145732
  286.8 22.6 %copy-start.12 = (f32[1024]{0:T(1024)S(1)}, f32[1024]{0:T(1024)}, u32[]{:S(2)}) copy-start(f32[1024]{0:T(1024)} %param.14) | copy-start | bytes 12292
  312.7 6.0 %collective-permute-start.3 = (bf16[6,3072]{1,0:T(8,128)(2,1)S(1)}, bf16[6,3072]{1,0:T(8,128)(2,1)S(1)}, u32[]{:S(2)}, u32[]{:S(2)}) collective-permute-start(bf16[6,3072]{1,0:T(8,128)(2,1)S(1)} %pad_maximum_fusion), channel_id=1, source_target_pairs={{2,0},{4,2},{6,4},{8,6},{10,8},{12,10},{14,12},{3,1},{5,3},{7,5},{... | collective-permute-start | bytes 110600 | tf_op jit(solution)/shard_map/ppermute | solution.py:14
  340.8 4.7 %copy-start.9 = (bf16[3,2,8,1024]{3,2,0,1:T(8,128)(2,1)S(1)}, bf16[3,2,8,1024]{3,2,0,1:T(8,128)(2,1)}, u32[]{:S(2)}) copy-start(bf16[3,2,8,1024]{3,2,0,1:T(8,128)(2,1)} %copy-done.8) | copy-start | bytes 294916
  345.5 2.9 copy-start.11
  358.1 84.4 %reduce-scatter.2.cloned.1.call-start = ((), (), s32[]{:S(2)}) async-start(), calls=%async_computation.2 | async-start | bytes 3145728 | tf_op jit(solution)/shard_map/reduce_scatter | solution.py:93
Sparse Core Ops, SparseCore 0:
  21.6 175.4 all-gather.1
  358.3 71.2 all-reduce.2
  432.4 10.0 reduce-scatter.1
where the time goes:
time: 455 us; the launch traced here: 449 us
  waiting for transfers between devices  251 us (55%)
  matrix products  88 us (19%)
  local copies, waits for them, and re-layouts  63.2 us (14%)
  other arithmetic  16.7 us (4%)
  between operations  14.3 us (3%)
  starting transfers between devices  11.8 us (3%)
    all_gather x1, waiting for transfers between devices, body(): lax.all_gather(merged, 'ctx', axis=0, tiled=True)  176 us
    psum x1, waiting for transfers between devices, body(): sum_a, sum_b = lax.psum((part_a, part_b), 'ctx')  59.5 us
    conv_general_dilated x2, matrix products, anticausal(): lax.conv_general_dilated(signal[None], filter_taps[:, None, :], (1,), 'VA...  28.6 us
    conv_general_dilated x2, matrix products, causal(): lax.conv_general_dilated(signal[None], filter_taps[::-1][:, None, :], (1,...  25.8 us
    conv_general_dilated x5, local copies, waits for them, and re-layouts, causal(): lax.conv_general_dilated(signal[None], filter_taps[::-1][:, None, :], (1,...  21.8 us
    dot_general x1, matrix products, body(): lax.dot_general(grad_packed, lax.all_gather(merged, 'ctx', axis=0, tiled=...  11.8 us
    ppermute x4, starting transfers between devices, shifted(): lax.ppermute(value, axis, [(source, source + steps) for source in range(i...  11.7 us
    reduce_scatter x1, waiting for transfers between devices, body(): lax.psum_scatter(partial_grad.astype(jnp.bfloat16), 'tp', scatter_dimensi...  9.77 us
  transfers between devices with their start and end apart: 7, of which 5 were waited for; matrix products, arithmetic and copies ran while one was open for 10% of the time, Pallas kernels for 0%

commit v1 on v0

v1 whole, which is shorter than its diff:
```python
import functools
import math

import jax
import jax.numpy as jnp
from jax import lax
from jax.experimental import pallas as pl
from jax.experimental.pallas import tpu as pltpu
from jax.sharding import PartitionSpec as P

adapter_scale = 0.03125
LANES = 128
SUB = 8
BLOCK = 16
CHUNK = 32


def shifted(value, axis, steps):
    count = lax.axis_size(axis)
    initial, last = (max(0, -steps), min(count, count - steps))
    return lax.ppermute(value, axis, [(source, source + steps) for source in range(initial, last)])


def tiles(ref, first, count):
    start = first * SUB
    if not isinstance(start, int):
        start = pl.multiple_of(start, SUB)
    return ref[pl.ds(start, count * SUB), :].reshape(count, SUB, LANES)


def put(ref, first, value):
    count = value.shape[0]
    ref[pl.ds(pl.multiple_of(first * SUB, SUB), count * SUB), :] = value.reshape(count * SUB, LANES)


def rounded(value):
    return value.astype(jnp.bfloat16).astype(jnp.float32)


def mixer_kernel(
    rows, halo, packed_ref, cot_ref, short_ref, long_ref, skip_ref, mixed_ref, grad_ref,
    p0, p1, p2, cot, query, keyed, valued, gated, gradf,
):
    channels = SUB * LANES
    short_taps = short_ref.shape[0] // 3
    long_taps = long_ref.shape[0]
    spread = (p0, p1, p2)
    front = halo - long_taps

    @pl.loop(0, (rows + 2 * halo) // BLOCK)
    def _(i):
        at = pl.multiple_of(i * BLOCK, BLOCK)
        for g in range(3):
            for s in range(SUB):
                piece = packed_ref[pl.ds(at, BLOCK), pl.ds(g * channels + s * LANES, LANES)]
                spread[g][pl.ds(at * SUB + s, BLOCK, stride=SUB), :] = piece.astype(jnp.float32)

    @pl.loop(0, (rows + halo) // BLOCK)
    def _(i):
        at = pl.multiple_of(i * BLOCK, BLOCK)
        for s in range(SUB):
            piece = cot_ref[pl.ds(at, BLOCK), pl.ds(s * LANES, LANES)]
            cot[pl.ds(at * SUB + s, BLOCK, stride=SUB), :] = piece.astype(jnp.float32)

    def short(ref, g, first, sign):
        total = None
        for j in range(short_taps):
            term = short_ref[j * 3 + g][None] * tiles(ref, first + sign * j, SUB)
            total = term if total is None else total + term
        return total

    @pl.loop(0, (rows + BLOCK + long_taps) // SUB)
    def _(i):
        at = i * SUB
        key = short(p1, 1, at + front, -1)
        val = short(p2, 2, at + front, -1)
        put(keyed, at, key)
        put(valued, at, val)
        put(gated, at, rounded(key * val))

    @pl.loop(0, (rows + halo) // SUB)
    def _(i):
        at = i * SUB
        que = short(p0, 0, at + halo, -1)
        put(query, at, que)
        put(gradf, at, rounded(que * tiles(cot, at, SUB)))

    zero = tuple(jnp.zeros((SUB, LANES), jnp.float32) for _ in range(BLOCK))

    def long_sum(ref, base, sign):
        def chunk(c, acc):
            acc = list(acc)
            tap0 = c * CHUNK
            origin = base + sign * tap0
            low = origin - (CHUNK - 1) if sign < 0 else origin
            seen = {}

            def at(k):
                if k not in seen:
                    seen[k] = ref[pl.ds(pl.multiple_of((low + k) * SUB, SUB), SUB), :]
                return seen[k]

            for j in range(CHUNK):
                tap = long_ref[tap0 + j]
                for i in range(BLOCK):
                    k = i + (CHUNK - 1) - j if sign < 0 else i + j
                    acc[i] = acc[i] + tap * at(k)
            return tuple(acc)

        return lax.fori_loop(0, long_taps // CHUNK, chunk, zero)

    @pl.loop(0, (rows + BLOCK) // BLOCK)
    def _(b):
        at = b * BLOCK
        skip = skip_ref[...]
        ahead = jnp.stack(long_sum(gated, at + long_taps, -1))
        filtered = ahead + skip[None] * tiles(gated, at + long_taps, BLOCK)
        back = jnp.stack(long_sum(gradf, at, 1))
        grad_gated = back + skip[None] * tiles(gradf, at, BLOCK)
        put(p0, at, rounded(tiles(cot, at, BLOCK) * filtered))
        put(p1, at, rounded(grad_gated * tiles(valued, at + long_taps, BLOCK)))
        put(p2, at, rounded(grad_gated * tiles(keyed, at + long_taps, BLOCK)))
        put(gated, at, tiles(query, at, BLOCK) * filtered)

    results = (query, keyed, valued)

    @pl.loop(0, rows // SUB)
    def _(i):
        at = i * SUB
        for g in range(3):
            put(results[g], at, short(spread[g], g, at, 1))

    @pl.loop(0, rows // BLOCK)
    def _(i):
        at = pl.multiple_of(i * BLOCK, BLOCK)
        for s in range(SUB):
            pick = pl.ds(at * SUB + s, BLOCK, stride=SUB)
            mixed_ref[pl.ds(at, BLOCK), pl.ds(s * LANES, LANES)] = gated[pick, :].astype(jnp.bfloat16)
            for g in range(3):
                grad_ref[pl.ds(at, BLOCK), pl.ds(g * channels + s * LANES, LANES)] = results[g][
                    pick, :
                ].astype(jnp.bfloat16)


def mixer(packed, cot, short_filter, long_filter, skip_gain, rows, halo):
    channels = long_filter.shape[1]
    long_taps = long_filter.shape[0]
    full = (rows + 2 * halo) * SUB
    side = (rows + halo) * SUB
    scratch = [pltpu.VMEM((full, LANES), jnp.float32)] * 3 + [
        pltpu.VMEM((side, LANES), jnp.float32)
    ] * 6
    return pl.pallas_call(
        functools.partial(mixer_kernel, rows, halo),
        out_shape=(
            jax.ShapeDtypeStruct((rows, channels), jnp.bfloat16),
            jax.ShapeDtypeStruct((rows, 3 * channels), jnp.bfloat16),
        ),
        in_specs=[pl.BlockSpec(memory_space=pltpu.VMEM)] * 5,
        out_specs=(pl.BlockSpec(memory_space=pltpu.VMEM),) * 2,
        scratch_shapes=scratch,
        compiler_params=pltpu.CompilerParams(vmem_limit_bytes=52 << 20),
        cost_estimate=pl.CostEstimate(
            flops=4 * rows * channels * (long_taps + 42), bytes_accessed=12 << 20, transcendentals=0
        ),
    )(
        packed,
        cot,
        short_filter.reshape(-1, SUB, LANES),
        long_filter.reshape(long_taps, SUB, LANES),
        skip_gain.reshape(SUB, LANES),
    )


def body(tokens, weight, adapter_a, adapter_b, short_filter, long_filter, skip_gain, cotangent):
    row_count = tokens.shape[0]
    share_rows = weight.shape[0]
    channels = weight.shape[2]
    features = tokens.shape[1]
    adapter_rank = adapter_a.shape[1]
    halo = long_filter.shape[0] + BLOCK
    seq_total = row_count * lax.axis_size("ctx")
    first_row = lax.axis_index("ctx") * share_rows
    before = shifted(tokens[row_count - halo :], "ctx", 1)
    after = shifted(tokens[:halo], "ctx", -1)
    cot_after = shifted(cotangent[:halo], "ctx", -1)
    tokens_ext = jnp.concatenate([before, tokens, after], axis=0)
    cot_ext = jnp.concatenate([cotangent, cot_after], axis=0)
    own_rows = lax.dynamic_slice_in_dim(adapter_a, first_row, share_rows, 0)
    flat_b = adapter_b.reshape(adapter_rank, 3 * channels)
    delta_w = jnp.dot(own_rows, flat_b, preferred_element_type=jnp.float32)
    merged = (
        weight.reshape(share_rows, 3 * channels).astype(jnp.float32) + adapter_scale * delta_w
    ).astype(jnp.bfloat16)
    whole = lax.all_gather(merged, "ctx", axis=0, tiled=True)
    packed = jnp.dot(tokens_ext, whole, preferred_element_type=jnp.float32).astype(jnp.bfloat16)
    mixed, grad_packed = mixer(
        packed, cot_ext, short_filter, long_filter, skip_gain, row_count, halo
    )
    projected = jnp.dot(tokens, adapter_a, preferred_element_type=jnp.float32).astype(jnp.bfloat16)
    part_b = lax.dot_general(
        projected, grad_packed, (((0,), (0,)), ((), ())), preferred_element_type=jnp.float32
    )
    through = lax.dot_general(
        flat_b, grad_packed, (((1,), (1,)), ((), ())), preferred_element_type=jnp.float32
    ).astype(jnp.bfloat16)
    part_a = jnp.dot(through, tokens, preferred_element_type=jnp.float32)
    mine = lax.axis_index("tp")
    spread_b = [jnp.where(mine == k, part_b, 0.0) for k in range(lax.axis_size("tp"))]
    sums = lax.psum(jnp.concatenate([part_a] + spread_b, axis=1), ("ctx", "tp"))
    sum_a = sums[:, :features].T
    sum_b = lax.dynamic_slice_in_dim(sums, features + mine * 3 * channels, 3 * channels, 1)
    partial_grad = lax.dot_general(
        grad_packed, whole, (((1,), (1,)), ((), ())), preferred_element_type=jnp.float32
    )
    grad_tokens = lax.psum_scatter(
        partial_grad.astype(jnp.bfloat16), "tp", scatter_dimension=1, tiled=True
    )
    factor = adapter_scale / math.sqrt(seq_total)
    return (mixed, grad_tokens, sum_a * factor, (sum_b * factor).reshape(adapter_rank, 3, channels))


def solution(mesh):
    return jax.shard_map(
        body,
        mesh=mesh,
        in_specs=(
            P(("groups", "ctx"), None),
            P("ctx", None, "tp"),
            P(),
            P(None, None, "tp"),
            P(None, None, "tp"),
            P(None, "tp"),
            P("tp"),
            P(("groups", "ctx"), "tp"),
        ),
        out_specs=(
            P(("groups", "ctx"), "tp"),
            P(("groups", "ctx"), "tp"),
            P("groups", None),
            P("groups", None, "tp"),
        ),
        check_vma=False,
    )
```

time: 455 us -> 401 us (0.88)
  Pallas kernels: 0 us -> 55.3 us
  local copies, waits for them, and re-layouts: 63.2 us -> 8.99 us
  matrix products: 88 us -> 39.4 us
  waiting for transfers between devices: 251 us -> 266 us
  other arithmetic: 16.7 us -> 6.09 us
    pallas_call x0 -> x1, Pallas kernels: none -> 55.3 us  [mixer(): pl.pallas_call(functools.partial(mixer_kernel, rows, halo), out_shape=(ja...]
    conv_general_dilated x4 -> x0, matrix products: 54.4 us -> none  [the longest x2 28.6 us: anticausal(): lax.conv_general_dilated(signal[None], filter_taps[:, None, :], (1,), 'VA...]
    all_gather x1, waiting for transfers between devices: 176 us -> 134 us  [body(): whole = lax.all_gather(merged, 'ctx', axis=0, tiled=True)]
    ppermute x4 -> x3, waiting for transfers between devices: 6.18 us -> 43.4 us  [shifted(): lax.ppermute(value, axis, [(source, source + steps) for source in range(i...]
    conv_general_dilated x8 -> x0, local copies, waits for them, and re-layouts: 30.3 us -> none  [the longest x5 21.8 us: causal(): lax.conv_general_dilated(signal[None], filter_taps[::-1][:, None, :], (1,...]
    psum x1, waiting for transfers between devices: 59.5 us -> 79 us  [body(): sums = lax.psum(jnp.concatenate([part_a] + spread_b, axis=1), ('ctx', 'tp'))]
    convert_element_type x2 -> x0, local copies, waits for them, and re-layouts: 8.25 us -> none  [body(): grad_packed = anticausal(jnp.concatenate([grad_short, later_short], axis=...]
    dot_general x4 -> x3, matrix products: 25.4 us -> 31.8 us  [the longest x1 15.7 us: body(): jnp.dot(tokens_ext, whole, preferred_element_type=jnp.float32)]
  transfers between devices with their start and end apart: 7 -> 6, of which waited for: 5 -> 4; matrix products, arithmetic and copies ran while one was open for 10% -> 5% of each run, Pallas kernels for 0% -> 0%
where the time goes in v1:
time: 401 us; the launch traced here: 399 us
  waiting for transfers between devices  266 us (66%)
  Pallas kernels  55.3 us (14%)
  matrix products  39.4 us (10%)
  between operations  13.9 us (3%)
  starting transfers between devices  9.27 us (2%)
  local copies, waits for them, and re-layouts  8.99 us (2%)
  other arithmetic  6.09 us (2%)
    all_gather x1, waiting for transfers between devices, body(): whole = lax.all_gather(merged, 'ctx', axis=0, tiled=True)  134 us
    psum x1, waiting for transfers between devices, body(): sums = lax.psum(jnp.concatenate([part_a] + spread_b, axis=1), ('ctx', 'tp'))  79 us
    pallas_call x1, Pallas kernels, mixer(): pl.pallas_call(functools.partial(mixer_kernel, rows, halo), out_shape=(ja...  55.3 us
    ppermute x3, waiting for transfers between devices, shifted(): lax.ppermute(value, axis, [(source, source + steps) for source in range(i...  43.4 us
    dot_general x1, matrix products, body(): jnp.dot(tokens_ext, whole, preferred_element_type=jnp.float32)  15.7 us
    dot_general x1, matrix products, body(): lax.dot_general(grad_packed, whole, (((1,), (1,)), ((), ())), preferred_e...  11.6 us
    reduce_scatter x1, waiting for transfers between devices, body(): lax.psum_scatter(partial_grad.astype(jnp.bfloat16), 'tp', scatter_dimensi...  9.58 us
    ppermute x3, starting transfers between devices, shifted(): lax.ppermute(value, axis, [(source, source + steps) for source in range(i...  9.14 us
  transfers between devices with their start and end apart: 6, of which 4 were waited for; matrix products, arithmetic and copies ran while one was open for 5% of the time, Pallas kernels for 0%

profile of v1, /device:TPU:24, one launch (start us, length us, event | category | flops | bytes accessed | tf_op | source)
XLA Modules:
  0.0 398.7 jit_solution(1512503349061697715)
XLA Ops:
  7.2 0.0 copy-start
  7.2 0.0 all-gather.2.cloned.1.call-start
  7.2 0.9 copy.21
  8.1 2.6 copy.15
  10.7 1.6 bitcast_convert_fusion
  12.4 2.3 copy.17
  14.7 3.8 fusion.1
  18.6 0.0 all-gather.2.cloned.1.call-update
  18.6 0.0 all-reduce.2.cloned.1.call-start
  18.6 1.1 fusion.13
  19.7 3.4 collective-permute-start
  23.1 3.3 collective-permute-start.1
  26.5 2.4 collective-permute-start.2
  28.9 1.2 copy.22
  30.2 0.1 copy.18
  30.3 43.4 %collective-permute-done.2 = bf16[144,1024]{1,0:T(8,128)(2,1)} collective-permute-done((bf16[144,1024]{1,0:T(8,128)(2,1)S(1)}, bf16[144,1024]{1,0:T(8,128)(2,1)}, u32[]{:S(2)}, u32[]{:S(2)}) %collective-permute-start.2) | collective-permute-done | bytes 294944 | tf_op jit(solution)/shard_map/ppermute | solution.py:21
  73.7 1.1 pad_maximum_fusion.cot_ref
  74.8 133.7 %all-gather.2.cloned.1.call-done = bf16[2048,3072]{1,0:T(8,128)(2,1)} async-done(((bf16[256,3072]{1,0:T(8,128)(2,1)}), bf16[2048,3072]{1,0:T(8,128)(2,1)}) %all-gather.2.cloned.1.call-update) | async-done | bytes 12582928 | tf_op jit(solution)/shard_map/all_gather | solution.py:195
  208.5 15.7 %convolution_convert_fusion.packed_ref = bf16[800,3072]{1,0:T(8,128)(2,1)} fusion(bf16[2048,3072]{1,0:T(8,128)(2,1)} %all-gather.2.cloned.1.call-done, bf16[144,2048]{1,0:T(8,128)(2,1)} %collective-permute-done.1, bf16[512,2048]{1,0:T(8,128)(2,1)} %param.8, bf16[144,2048]{1,0:T(8,128)(2,1)} %collective-permute-done), kind=kOutput, calls=%fused_computation | convolution fusion | flops 10078617600 | bytes 20774912 | tf_op jit(solution)/shard_map/dot_general | solution.py:196
  224.2 55.3 %shard_map.111 = (bf16[512,1024]{1,0:T(8,128)(2,1)}, bf16[512,3072]{1,0:T(8,128)(2,1)}) custom-call(bf16[800,3072]{1,0:T(8,128)(2,1)} %convolution_convert_fusion.packed_ref, bf16[656,1024]{1,0:T(8,128)(2,1)S(1)} %pad_maximum_fusion.cot_ref, f32[21,8,128]{2,1,0:T(8,128)S(1)} %reshape.27.short_ref, f32[128,8,128]{2,1,0:T(8,128)S(1)} %bitcast.24, ...), custom_call_target="tpu_custom_call" | custom-call | flops 356515840 | bytes 12582912 | tf_op jit(solution)/shard_map/pallas_call | solution.py:153
  279.4 4.5 %fusion.7 = f32[16,2048]{1,0:T(8,128)S(1)} fusion(bf16[512,2048]{1,0:T(8,128)(2,1)} %param.8, bf16[512,3072]{1,0:T(8,128)(2,1)} %get-tuple-element.7, bf16[16,3072]{1,0:T(8,128)(2,1)S(1)} %bitcast.27), kind=kOutput, calls=%fused_computation.14 | convolution fusion | flops 83894272 | bytes 5472256 | tf_op jit(solution)/shard_map/dot_general | solution.py:207
  283.9 3.8 broadcast_select_fusion.1
  287.7 0.9 pad_maximum_fusion.1
  288.6 0.0 all-reduce.2.cloned.1.call-update
  288.6 0.0 reduce-scatter.2.cloned.1.call-start
  288.7 11.6 %convolution_convert_fusion.1 = bf16[512,2048]{1,0:T(8,128)(2,1)} fusion(bf16[512,3072]{1,0:T(8,128)(2,1)} %get-tuple-element.7, bf16[2048,3072]{1,0:T(8,128)(2,1)} %all-gather.2.cloned.1.call-done), kind=kOutput, calls=%fused_computation.9 | convolution fusion | flops 6443499520 | bytes 17825792 | tf_op jit(solution)/shard_map/dot_general | solution.py:213
  300.3 0.0 reduce-scatter.2.cloned.1.call-update
  300.4 79.0 %all-reduce.2.cloned.1.call-done = f32[16,8192]{1,0:T(8,128)} async-done(((f32[16,8192]{1,0:T(8,128)}), f32[16,8192]{1,0:T(8,128)}) %all-reduce.2.cloned.1.call-update) | async-done | bytes 524304 | tf_op jit(solution)/shard_map/psum | solution.py:210
  379.4 0.9 dynamic-slice_multiply_fusion
  380.3 0.7 copy.24
  381.0 1.6 fusion.9
  382.6 9.6 %reduce-scatter.2.cloned.1.call-done = bf16[512,1024]{1,0:T(8,128)(2,1)} async-done(((bf16[512,2048]{1,0:T(8,128)(2,1)}), bf16[512,1024]{1,0:T(8,128)(2,1)}) %reduce-scatter.2.cloned.1.call-update) | async-done | bytes 1048592 | tf_op jit(solution)/shard_map/reduce_scatter | solution.py:216
  (15 shorter events, 0.1 us)
Async XLA Ops:
  7.2 7.6 %copy-start = (bf16[2048,16]{0,1:T(8,128)(2,1)S(1)}, bf16[2048,16]{0,1:T(8,128)(2,1)}, u32[]{:S(2)}) copy-start(bf16[2048,16]{0,1:T(8,128)(2,1)} %param.10) | copy-start | bytes 196612
  7.2 201.3 %all-gather.2.cloned.1.call-start = ((), (), s32[]{:S(2)}) async-start(), calls=%async_computation.1 | async-start | bytes 14155776 | tf_op jit(solution)/shard_map/all_gather | solution.py:195
  14.7 3.9 copy-start.2
  18.5 7.9 %copy-start.4 = (bf16[512,1024]{1,0:T(8,128)(2,1)S(1)}, bf16[512,1024]{1,0:T(8,128)(2,1)}, u32[]{:S(2)}) copy-start(bf16[512,1024]{1,0:T(8,128)(2,1)} %param.15) | copy-start | bytes 3145732
  18.6 11.6 %copy-start.5 = (f32[7,3,1024]{2,0,1:T(8,128)S(1)}, f32[7,3,1024]{2,0,1:T(8,128)}, u32[]{:S(2)}) copy-start(f32[7,3,1024]{2,0,1:T(8,128)} %param.12) | copy-start | bytes 258052
  18.6 360.8 %all-reduce.2.cloned.1.call-start = ((), (), s32[]{:S(2)}) async-start(), calls=%async_computation.3 | async-start | bytes 1048576 | tf_op jit(solution)/shard_map/psum | solution.py:210
  19.7 55.0 %collective-permute-start = (bf16[144,2048]{1,0:T(8,128)(2,1)}, bf16[144,2048]{1,0:T(8,128)(2,1)}, u32[]{:S(2)}, u32[]{:S(2)}) collective-permute-start(bf16[144,2048]{1,0:T(8,128)(2,1)} %get-tuple-element.16), channel_id=1, source_target_pairs={{0,2},{2,4},{4,6},{6,8},{8,10},{10,12},{12,14},{1,3},{3,5},{5,7},{... | collective-permute-start | bytes 1769480 | tf_op jit(solution)/shard_map/ppermute | solution.py:21
  23.1 51.6 %collective-permute-start.1 = (bf16[144,2048]{1,0:T(8,128)(2,1)}, bf16[144,2048]{1,0:T(8,128)(2,1)}, u32[]{:S(2)}, u32[]{:S(2)}) collective-permute-start(bf16[144,2048]{1,0:T(8,128)(2,1)} %get-tuple-element.17), channel_id=1, source_target_pairs={{2,0},{4,2},{6,4},{8,6},{10,8},{12,10},{14,12},{3,1},{5,3},{7,5},{... | collective-permute-start | bytes 1769480 | tf_op jit(solution)/shard_map/ppermute | solution.py:21
  26.5 47.2 %collective-permute-start.2 = (bf16[144,1024]{1,0:T(8,128)(2,1)S(1)}, bf16[144,1024]{1,0:T(8,128)(2,1)}, u32[]{:S(2)}, u32[]{:S(2)}) collective-permute-start(bf16[144,1024]{1,0:T(8,128)(2,1)S(1)} %slice.14), channel_id=1, source_target_pairs={{2,0},{4,2},{6,4},{8,6},{10,8},{12,10},{14,12},{3,1},{5,3},{7,5},{... | collective-permute-start | bytes 884744 | tf_op jit(solution)/shard_map/ppermute | solution.py:21
  74.8 149.4 %copy-start.1 = (f32[1024]{0:T(1024)S(1)}, f32[1024]{0:T(1024)}, u32[]{:S(2)}) copy-start(f32[1024]{0:T(1024)} %param.14) | copy-start | bytes 12292
  279.4 4.5 %copy-start.3 = (bf16[512,2048]{1,0:T(8,128)(2,1)S(1)}, bf16[512,2048]{1,0:T(8,128)(2,1)}, u32[]{:S(2)}) copy-start(bf16[512,2048]{1,0:T(8,128)(2,1)} %param.8) | copy-start | bytes 6291460
  288.6 103.5 %reduce-scatter.2.cloned.1.call-start = ((), (), s32[]{:S(2)}) async-start(), calls=%async_computation.2 | async-start | bytes 3145728 | tf_op jit(solution)/shard_map/reduce_scatter | solution.py:216
Sparse Core Ops, SparseCore 0:
  18.7 189.7 all-gather.1
  288.7 90.5 all-reduce.1
  382.2 9.9 reduce-scatter.1

commit v2 on v1

--- a/solution.py
+++ b/solution.py
@@ -169,6 +169,159 @@
         short_filter.reshape(-1, SUB, LANES),
         long_filter.reshape(long_taps, SUB, LANES),
         skip_gain.reshape(SUB, LANES),
+    )
+
+
+def finish_kernel(
+    count, grad_ref, whole_ref, terms_ref, tokens_ref, sums_ref,
+    held, total, mate, summed, ready, landed,
+    send_one, recv_one, send_two, recv_two, send_tp, recv_tp, send_tok, recv_tok,
+):
+    me = lax.axis_index("ctx")
+    mine = lax.axis_index("tp")
+    other = 1 - mine
+    width = mate.shape[1]
+    cols = tokens_ref.shape[1]
+    tile = ready.shape[2]
+    steps = cols // tile
+
+    barrier = pltpu.get_barrier_semaphore()
+    for d in range(1, count):
+        pl.semaphore_signal(
+            barrier, inc=1, device_id={"ctx": lax.rem(me + d, count)}, device_id_type=pl.DeviceIdType.MESH
+        )
+    pl.semaphore_signal(barrier, inc=1, device_id={"tp": other}, device_id_type=pl.DeviceIdType.MESH)
+    pl.semaphore_wait(barrier, count)
+
+    first = []
+    for d in range(1, count):
+        peer = lax.rem(me + d, count)
+        first.append(
+            pltpu.make_async_remote_copy(
+                src_ref=terms_ref.at[peer],
+                dst_ref=held.at[d],
+                send_sem=send_one.at[d],
+                recv_sem=recv_one.at[d],
+                device_id={"ctx": peer},
+                device_id_type=pl.DeviceIdType.MESH,
+            )
+        )
+        first[-1].start()
+
+    def product(half, t):
+        at = pl.multiple_of(half * cols + t * tile, tile)
+        return lax.dot_general(
+            grad_ref[...],
+            whole_ref[pl.ds(at, tile), :],
+            (((1,), (1,)), ((), ())),
+            preferred_element_type=jnp.float32,
+        )
+
+    def token_copy(t):
+        return pltpu.make_async_remote_copy(
+            src_ref=ready.at[t],
+            dst_ref=landed.at[t],
+            send_sem=send_tok.at[t],
+            recv_sem=recv_tok.at[t],
+            device_id={"tp": other},
+            device_id_type=pl.DeviceIdType.MESH,
+        )
+
+    @pl.loop(0, steps)
+    def _(t):
+        ready[t] = product(other, t).astype(jnp.bfloat16)
+        token_copy(t).start()
+
+    own = terms_ref[me]
+    for d in range(1, count):
+        first[d - 1].wait()
+        own = own + held[d]
+    total[...] = own
+    tp_copy = pltpu.make_async_remote_copy(
+        src_ref=total.at[:, pl.ds(0, width)],
+        dst_ref=mate,
+        send_sem=send_tp,
+        recv_sem=recv_tp,
+        device_id={"tp": other},
+        device_id_type=pl.DeviceIdType.MESH,
+    )
+    tp_copy.start()
+
+    def own_tile(t):
+        value = product(mine, t)
+        token_copy(t).wait()
+        at = pl.multiple_of(t * tile, tile)
+        tokens_ref[:, pl.ds(at, tile)] = (value + landed[t].astype(jnp.float32)).astype(jnp.bfloat16)
+
+    pl.loop(0, steps // 4)(own_tile)
+    tp_copy.wait()
+    total[:, pl.ds(0, width)] = total[:, pl.ds(0, width)] + mate[...]
+    summed[me] = total[...]
+    second = []
+    for d in range(1, count):
+        second.append(
+            pltpu.make_async_remote_copy(
+                src_ref=total,
+                dst_ref=summed.at[me],
+                send_sem=send_two.at[d],
+                recv_sem=recv_two.at[d],
+                device_id={"ctx": lax.rem(me + d, count)},
+                device_id_type=pl.DeviceIdType.MESH,
+            )
+        )
+        second[-1].start()
+    pl.loop(steps // 4, steps)(own_tile)
+    for copy in second:
+        copy.wait()
+    sums_ref[...] = summed[...]
+
+
+def finish(grad_packed, whole, part_a, part_b, count):
+    rank, features = part_a.shape
+    rows, wide = grad_packed.shape
+    width, rest = features // count, wide // count
+    cols = features // 2
+    tile = 256
+    terms = jnp.concatenate(
+        [part_a.reshape(rank, count, width), part_b.reshape(rank, count, rest)], axis=2
+    ).transpose(1, 0, 2)
+    vmem = pl.BlockSpec(memory_space=pltpu.VMEM)
+    grad_tokens, sums = pl.pallas_call(
+        functools.partial(finish_kernel, count),
+        out_shape=(
+            jax.ShapeDtypeStruct((rows, cols), jnp.bfloat16),
+            jax.ShapeDtypeStruct(terms.shape, jnp.float32),
+        ),
+        in_specs=[vmem] * 3,
+        out_specs=(vmem, vmem),
+        scratch_shapes=[
+            pltpu.VMEM(terms.shape, jnp.float32),
+            pltpu.VMEM((rank, width + rest), jnp.float32),
+            pltpu.VMEM((rank, width), jnp.float32),
+            pltpu.VMEM(terms.shape, jnp.float32),
+            pltpu.VMEM((cols // tile, rows, tile), jnp.bfloat16),
+            pltpu.VMEM((cols // tile, rows, tile), jnp.bfloat16),
+            pltpu.SemaphoreType.DMA((count,)),
+            pltpu.SemaphoreType.DMA((count,)),
+            pltpu.SemaphoreType.DMA((count,)),
+            pltpu.SemaphoreType.DMA((count,)),
+            pltpu.SemaphoreType.DMA,
+            pltpu.SemaphoreType.DMA,
+            pltpu.SemaphoreType.DMA((cols // tile,)),
+            pltpu.SemaphoreType.DMA((cols // tile,)),
+        ],
+        compiler_params=pltpu.CompilerParams(
+            vmem_limit_bytes=48 << 20, collective_id=1, has_side_effects=True
+        ),
+        cost_estimate=pl.CostEstimate(
+            flops=2 * rows * wide * features, bytes_accessed=20 << 20, transcendentals=0
+        ),
+    )(grad_packed, whole, terms)
+    flat = sums.transpose(1, 0, 2)
+    return (
+        grad_tokens,
+        flat[:, :, :width].reshape(rank, features),
+        flat[:, :, width:].reshape(rank, wide),
     )
 
 
@@ -205,17 +358,19 @@
         flat_b, grad_packed, (((1,), (1,)), ((), ())), preferred_element_type=jnp.float32
     ).astype(jnp.bfloat16)
     part_a = jnp.dot(through, tokens, preferred_element_type=jnp.float32)
-    mine = lax.axis_index("tp")
-    spread_b = [jnp.where(mine == k, part_b, 0.0) for k in range(lax.axis_size("tp"))]
-    sums = lax.psum(jnp.concatenate([part_a] + spread_b, axis=1), ("ctx", "tp"))
-    sum_a = sums[:, :features].T
-    sum_b = lax.dynamic_slice_in_dim(sums, features + mine * 3 * channels, 3 * channels, 1)
-    partial_grad = lax.dot_general(
-        grad_packed, whole, (((1,), (1,)), ((), ())), preferred_element_type=jnp.float32
-    )
-    grad_tokens = lax.psum_scatter(
-        partial_grad.astype(jnp.bfloat16), "tp", scatter_dimension=1, tiled=True
-    )
+    count = lax.axis_size("ctx")
+    if features % (LANES * count) == 0 and (3 * channels) % (LANES * count) == 0:
+        grad_tokens, sum_a, sum_b = finish(grad_packed, whole, part_a, part_b, count)
+    else:
+        sum_a = lax.psum(part_a, ("ctx", "tp"))
+        sum_b = lax.psum(part_b, "ctx")
+        partial_grad = lax.dot_general(
+            grad_packed, whole, (((1,), (1,)), ((), ())), preferred_element_type=jnp.float32
+        )
+        grad_tokens = lax.psum_scatter(
+            partial_grad.astype(jnp.bfloat16), "tp", scatter_dimension=1, tiled=True
+        )
+    sum_a = sum_a.T
     factor = adapter_scale / math.sqrt(seq_total)
     return (mixed, grad_tokens, sum_a * factor, (sum_b * factor).reshape(adapter_rank, 3, channels))
 

time: 401 us -> 326 us (0.81)
  waiting for transfers between devices: 266 us -> 177 us
  Pallas kernels: 55.3 us -> 81.3 us
  matrix products: 39.4 us -> 27.5 us
  local copies, waits for them, and re-layouts: 8.99 us -> 13.2 us
    psum x1 -> x0, waiting for transfers between devices: 79 us -> none  [body(): sums = lax.psum(jnp.concatenate([part_a] + spread_b, axis=1), ('ctx', 'tp'))]
    pallas_call x0 -> x1, Pallas kernels: none -> 26 us  [finish(): pl.pallas_call(functools.partial(finish_kernel, count), out_shape=(jax.Sh...]
    dot_general x1 -> x0, matrix products: 11.6 us -> none  [body(): lax.dot_general(grad_packed, whole, (((1,), (1,)), ((), ())), preferred_e...]
    reduce_scatter x1 -> x0, waiting for transfers between devices: 9.58 us -> none  [body(): lax.psum_scatter(partial_grad.astype(jnp.bfloat16), 'tp', scatter_dimensi...]
    unnamed x15 -> x19, local copies, waits for them, and re-layouts: 3.9 us -> 7.91 us
  transfers between devices with their start and end apart: 6 -> 4, of which waited for: 4 -> 2; matrix products, arithmetic and copies ran while one was open for 5% -> 1% of each run, Pallas kernels for 0% -> 0%
where the time goes in v2:
time: 326 us; the launch traced here: 325 us
  waiting for transfers between devices  177 us (54%)
  Pallas kernels  81.3 us (25%)
  matrix products  27.5 us (8%)
  between operations  14.2 us (4%)
  local copies, waits for them, and re-layouts  13.2 us (4%)
  starting transfers between devices  9.19 us (3%)
    all_gather x1, waiting for transfers between devices, body(): whole = lax.all_gather(merged, 'ctx', axis=0, tiled=True)  134 us
    pallas_call x1, Pallas kernels, mixer(): pl.pallas_call(functools.partial(mixer_kernel, rows, halo), out_shape=(ja...  55.3 us
    ppermute x3, waiting for transfers between devices, shifted(): lax.ppermute(value, axis, [(source, source + steps) for source in range(i...  43.4 us
    pallas_call x1, Pallas kernels, finish(): pl.pallas_call(functools.partial(finish_kernel, count), out_shape=(jax.Sh...  26 us
    dot_general x1, matrix products, body(): jnp.dot(tokens_ext, whole, preferred_element_type=jnp.float32)  15.6 us
    ppermute x3, starting transfers between devices, shifted(): lax.ppermute(value, axis, [(source, source + steps) for source in range(i...  9.15 us
    unnamed x19, local copies, waits for them, and re-layouts  7.91 us
  transfers between devices with their start and end apart: 4, of which 2 were waited for; matrix products, arithmetic and copies ran while one was open for 1% of the time, Pallas kernels for 0%

profile of v2, /device:TPU:24, one launch (start us, length us, event | category | flops | bytes accessed | tf_op | source)
XLA Modules:
  0.0 325.2 jit_solution(970769613754595055)
XLA Ops:
  7.2 0.0 copy-start
  7.2 0.0 all-gather.2.cloned.1.call-start
  7.2 0.9 copy.25
  8.1 2.6 copy.14
  10.7 1.6 bitcast_convert_fusion
  12.4 2.3 copy.16
  14.7 0.0 copy-done
  14.7 3.8 %fusion.1 = bf16[256,3072]{1,0:T(8,128)(2,1)} fusion(f32[256,3072]{1,0:T(8,128)} %copy.16, bf16[16,3072]{1,0:T(8,128)(2,1)S(1)} %bitcast.36, bf16[2048,16]{0,1:T(8,128)(2,1)S(1)} %copy-done, s32[]{:T(128)S(6)} %select_n.3), kind=kOutput, calls=%fused_computation.3 | convolution fusion | flops 27525120 | bytes 4825092 | tf_op jit(solution)/shard_map/dot_general | solution.py:344
  18.5 0.0 all-gather.2.cloned.1.call-update
  18.6 1.1 fusion.13
  19.7 3.4 %collective-permute-start = (bf16[144,2048]{1,0:T(8,128)(2,1)}, bf16[144,2048]{1,0:T(8,128)(2,1)}, u32[]{:S(2)}, u32[]{:S(2)}) collective-permute-start(bf16[144,2048]{1,0:T(8,128)(2,1)} %get-tuple-element.16), channel_id=1, source_target_pairs={{0,2},{2,4},{4,6},{6,8},{8,10},{10,12},{12,14},{1,3},{3,5},{5,7},{... | collective-permute-start | bytes 1769480 | tf_op jit(solution)/shard_map/ppermute | solution.py:21
  23.1 3.3 %collective-permute-start.1 = (bf16[144,2048]{1,0:T(8,128)(2,1)}, bf16[144,2048]{1,0:T(8,128)(2,1)}, u32[]{:S(2)}, u32[]{:S(2)}) collective-permute-start(bf16[144,2048]{1,0:T(8,128)(2,1)} %get-tuple-element.17), channel_id=1, source_target_pairs={{2,0},{4,2},{6,4},{8,6},{10,8},{12,10},{14,12},{3,1},{5,3},{7,5},{... | collective-permute-start | bytes 1769480 | tf_op jit(solution)/shard_map/ppermute | solution.py:21
  26.5 2.4 collective-permute-start.2
  28.9 0.1 copy.17
  29.0 1.2 copy.27
  30.2 43.4 %collective-permute-done.2 = bf16[144,1024]{1,0:T(8,128)(2,1)} collective-permute-done((bf16[144,1024]{1,0:T(8,128)(2,1)S(1)}, bf16[144,1024]{1,0:T(8,128)(2,1)}, u32[]{:S(2)}, u32[]{:S(2)}) %collective-permute-start.2) | collective-permute-done | bytes 294944 | tf_op jit(solution)/shard_map/ppermute | solution.py:21
  73.6 1.1 pad_maximum_fusion.cot_ref
  74.7 0.0 copy-start.3
  74.7 0.0 collective-permute-done
  74.7 0.0 collective-permute-done.1
  74.7 133.7 %all-gather.2.cloned.1.call-done.whole_ref = bf16[2048,3072]{1,0:T(8,128)(2,1)} async-done(((bf16[256,3072]{1,0:T(8,128)(2,1)}), bf16[2048,3072]{1,0:T(8,128)(2,1)}) %all-gather.2.cloned.1.call-update) | async-done | bytes 12582928 | tf_op jit(solution)/shard_map/all_gather | solution.py:348
  208.4 15.6 %convolution_convert_fusion.packed_ref = bf16[800,3072]{1,0:T(8,128)(2,1)} fusion(bf16[2048,3072]{1,0:T(8,128)(2,1)} %all-gather.2.cloned.1.call-done.whole_ref, bf16[144,2048]{1,0:T(8,128)(2,1)} %collective-permute-done.1, bf16[512,2048]{1,0:T(8,128)(2,1)} %param.8, bf16[144,2048]{1,0:T(8,128)(2,1)} %collective-permute-done), kind=kOutput, calls=%fused_computation | convolution fusion | flops 10078617600 | bytes 20774912 | tf_op jit(solution)/shard_map/dot_general | solution.py:349
  224.1 55.3 %shard_map.111 = (bf16[512,1024]{1,0:T(8,128)(2,1)}, bf16[512,3072]{1,0:T(8,128)(2,1)}) custom-call(bf16[800,3072]{1,0:T(8,128)(2,1)} %convolution_convert_fusion.packed_ref, bf16[656,1024]{1,0:T(8,128)(2,1)S(1)} %pad_maximum_fusion.cot_ref, f32[21,8,128]{2,1,0:T(8,128)S(1)} %reshape.38.short_ref, f32[128,8,128]{2,1,0:T(8,128)S(1)} %bitcast.32, ...), custom_call_target="tpu_custom_call" | custom-call | flops 356515840 | bytes 12582912 | tf_op jit(solution)/shard_map/pallas_call | solution.py:153
  279.4 4.5 %fusion.7 = f32[16,2048]{1,0:T(8,128)S(1)} fusion(bf16[512,2048]{1,0:T(8,128)(2,1)} %param.8, bf16[512,3072]{1,0:T(8,128)(2,1)} %get-tuple-element.9.grad_ref, bf16[16,3072]{1,0:T(8,128)(2,1)S(1)} %bitcast.37), kind=kOutput, calls=%fused_computation.13 | convolution fusion | flops 83894272 | bytes 5472256 | tf_op jit(solution)/shard_map/dot_general | solution.py:360
  283.9 3.5 %fusion.8 = f32[16,3072]{1,0:T(8,128)S(1)} fusion(bf16[512,3072]{1,0:T(8,128)(2,1)S(1)} %copy-done.1, bf16[512,2048]{1,0:T(8,128)(2,1)} %param.8, bf16[2048,16]{0,1:T(8,128)(2,1)S(1)} %copy-done), kind=kOutput, calls=%fused_computation.14 | convolution fusion | flops 83894272 | bytes 5505024 | tf_op jit(solution)/shard_map/dot_general | solution.py:354
  287.5 26.0 %shard_map.112 = (bf16[512,1024]{1,0:T(8,128)(2,1)S(1)}, f32[8,16,640]{2,1,0:T(8,128)S(1)}) custom-call(bf16[512,3072]{1,0:T(8,128)(2,1)S(1)} %copy-done.1, bf16[2048,3072]{1,0:T(8,128)(2,1)} %all-gather.2.cloned.1.call-done.whole_ref, f32[8,16,640]{2,1,0:T(8,128)S(1)} %maximum_bitcast_fusion.terms_ref), custom_call_target="tpu_custom_call" | custom-call | flops 6442450944 | bytes 20971520 | tf_op jit(solution)/shard_map/pallas_call | solution.py:289
  313.5 1.0 copy-done.2
  314.5 0.1 copy.21
  314.6 0.7 copy.26
  315.2 0.1 mul.40
  315.3 0.8 copy.22
  316.1 2.3 copy.33
  (17 shorter events, 0.2 us)
Async XLA Ops:
  7.2 7.6 %copy-start = (bf16[2048,16]{0,1:T(8,128)(2,1)S(1)}, bf16[2048,16]{0,1:T(8,128)(2,1)}, u32[]{:S(2)}) copy-start(bf16[2048,16]{0,1:T(8,128)(2,1)} %param.10) | copy-start | bytes 196612
  7.2 201.3 %all-gather.2.cloned.1.call-start = ((), (), s32[]{:S(2)}) async-start(), calls=%async_computation | async-start | bytes 14155776 | tf_op jit(solution)/shard_map/all_gather | solution.py:348
  14.7 3.8 %copy-start.4 = (bf16[512,2048]{1,0:T(8,128)(2,1)S(1)}, bf16[512,2048]{1,0:T(8,128)(2,1)}, u32[]{:S(2)}) copy-start(bf16[512,2048]{1,0:T(8,128)(2,1)} %param.8) | copy-start | bytes 6291460
  18.5 7.9 %copy-start.5 = (bf16[512,1024]{1,0:T(8,128)(2,1)S(1)}, bf16[512,1024]{1,0:T(8,128)(2,1)}, u32[]{:S(2)}) copy-start(bf16[512,1024]{1,0:T(8,128)(2,1)} %param.15) | copy-start | bytes 3145732
  18.5 10.3 %copy-start.6 = (f32[7,3,1024]{2,0,1:T(8,128)S(1)}, f32[7,3,1024]{2,0,1:T(8,128)}, u32[]{:S(2)}) copy-start(f32[7,3,1024]{2,0,1:T(8,128)} %param.12) | copy-start | bytes 258052
  19.7 55.1 %collective-permute-start = (bf16[144,2048]{1,0:T(8,128)(2,1)}, bf16[144,2048]{1,0:T(8,128)(2,1)}, u32[]{:S(2)}, u32[]{:S(2)}) collective-permute-start(bf16[144,2048]{1,0:T(8,128)(2,1)} %get-tuple-element.16), channel_id=1, source_target_pairs={{0,2},{2,4},{4,6},{6,8},{8,10},{10,12},{12,14},{1,3},{3,5},{5,7},{... | collective-permute-start | bytes 1769480 | tf_op jit(solution)/shard_map/ppermute | solution.py:21
  23.1 51.6 %collective-permute-start.1 = (bf16[144,2048]{1,0:T(8,128)(2,1)}, bf16[144,2048]{1,0:T(8,128)(2,1)}, u32[]{:S(2)}, u32[]{:S(2)}) collective-permute-start(bf16[144,2048]{1,0:T(8,128)(2,1)} %get-tuple-element.17), channel_id=1, source_target_pairs={{2,0},{4,2},{6,4},{8,6},{10,8},{12,10},{14,12},{3,1},{5,3},{7,5},{... | collective-permute-start | bytes 1769480 | tf_op jit(solution)/shard_map/ppermute | solution.py:21
  26.5 47.2 %collective-permute-start.2 = (bf16[144,1024]{1,0:T(8,128)(2,1)S(1)}, bf16[144,1024]{1,0:T(8,128)(2,1)}, u32[]{:S(2)}, u32[]{:S(2)}) collective-permute-start(bf16[144,1024]{1,0:T(8,128)(2,1)S(1)} %slice.17), channel_id=1, source_target_pairs={{2,0},{4,2},{6,4},{8,6},{10,8},{12,10},{14,12},{3,1},{5,3},{7,5},{... | collective-permute-start | bytes 884744 | tf_op jit(solution)/shard_map/ppermute | solution.py:21
  74.7 149.4 %copy-start.3 = (f32[1024]{0:T(1024)S(1)}, f32[1024]{0:T(1024)}, u32[]{:S(2)}) copy-start(f32[1024]{0:T(1024)} %param.14) | copy-start | bytes 12292
  279.4 4.5 %copy-start.1 = (bf16[512,3072]{1,0:T(8,128)(2,1)S(1)}, bf16[512,3072]{1,0:T(8,128)(2,1)}, u32[]{:S(2)}) copy-start(bf16[512,3072]{1,0:T(8,128)(2,1)} %get-tuple-element.9.grad_ref) | copy-start | bytes 9437188
  313.5 1.0 copy-start.2
Sparse Core Ops, SparseCore 0:
  18.7 189.7 all-gather.1

commit v3 on v2

--- a/solution.py
+++ b/solution.py
@@ -325,6 +325,197 @@
     )
 
 
+MESH = pl.DeviceIdType.MESH
+PIECES = 4
+
+
+def gather_kernel(
+    outer, shard_ref, out_ref, z_send, z_recv, y_send, y_recv, x_send, x_recv, local_sem
+):
+    me = lax.axis_index("ctx")
+    x = lax.axis_index("groups")
+    z, y = me // 2, lax.rem(me, 2)
+    rows = shard_ref.shape[0]
+    piece = rows // PIECES
+    half = piece // 2
+    last = outer - 2
+    steps = outer - 1
+
+    def ctx_of(line, pair):
+        return {"ctx": line * 2 + pair}
+
+    def span(line, pair, start, size):
+        return pl.ds(pl.multiple_of((line * 2 + pair) * rows + start, half), size)
+
+    def part(p, side):
+        return p * piece + side * half
+
+    def copy(src, dst, send, recv, device):
+        return pltpu.make_async_remote_copy(
+            src_ref=src, dst_ref=dst, send_sem=send, recv_sem=recv, device_id=device, device_id_type=MESH
+        )
+
+    def z_range(k, p):
+        return (part(p, x), half) if k == last else (p * piece, piece)
+
+    def z_out(way, k, p):
+        step = 1 - 2 * way
+        start, size = z_range(k, p)
+        place = span(z - step * k, y, start, size)
+        src = out_ref.at[place] if k else shard_ref.at[pl.ds(pl.multiple_of(start, half), size)]
+        return copy(
+            src, out_ref.at[place], z_send.at[way, k, p], z_recv.at[way, k, p], ctx_of(z + step, y)
+        )
+
+    def z_in(way, k, p):
+        step = 1 - 2 * way
+        start, size = z_range(k, p)
+        place = out_ref.at[span(z - step * (k + 1), y, start, size)]
+        return copy(place, place, z_send.at[way, k, p], z_recv.at[way, k, p], ctx_of(z - step, y))
+
+    def sends(way, k):
+        return (z < steps) & (z >= k) if way == 0 else (z > 0) & (z + k <= steps)
+
+    def receives(way, k):
+        return z > k if way == 0 else z + k < steps
+
+    def line_of(i):
+        if i == 0:
+            return z
+        way, k = (i - 1) // steps, (i - 1) % steps
+        return z - (1 - 2 * way) * (k + 1)
+
+    def item(way, k):
+        return 1 + way * steps + k
+
+    def y_out(i, p):
+        start = part(p, x)
+        place = span(line_of(i), y, start, half)
+        src = out_ref.at[place] if i else shard_ref.at[pl.ds(pl.multiple_of(start, half), half)]
+        return copy(src, out_ref.at[place], y_send.at[i, p], y_recv.at[i, p], ctx_of(z, 1 - y))
+
+    def y_in(i, p):
+        place = out_ref.at[span(line_of(i), 1 - y, part(p, x), half)]
+        return copy(place, place, y_send.at[i, p], y_recv.at[i, p], ctx_of(z, 1 - y))
+
+    def x_copy(i, p, side):
+        if i > 2 * steps:
+            line, pair = line_of(item(i - 2 * steps - 1, last)), y
+        else:
+            line, pair = line_of(i), 1 - y
+        place = out_ref.at[span(line, pair, part(p, side), half)]
+        return copy(place, place, x_send.at[i, p], x_recv.at[i, p], {"groups": 1 - x})
+
+    def extra(way):
+        return 2 * steps + 1 + way
+
+    barrier = pltpu.get_barrier_semaphore()
+    pl.semaphore_signal(barrier, inc=1, device_id=ctx_of(z, 1 - y), device_id_type=MESH)
+    pl.semaphore_signal(barrier, inc=1, device_id={"groups": 1 - x}, device_id_type=MESH)
+    for step in (1, outer - 1):
+        pl.semaphore_signal(
+            barrier, inc=1, device_id=ctx_of(lax.rem(z + step, outer), y), device_id_type=MESH
+        )
+    pl.semaphore_wait(barrier, 4)
+
+    @pl.loop(0, PIECES)
+    def _(p):
+        for way in range(2):
+            @pl.when(sends(way, 0))
+            def _():
+                z_out(way, 0, p).start()
+        y_out(0, p).start()
+
+    own = pltpu.make_async_copy(
+        shard_ref, out_ref.at[pl.ds(pl.multiple_of(me * rows, rows), rows)], local_sem
+    )
+    own.start()
+
+    def pass_on(k, p):
+        for way in range(2):
+            @pl.when(receives(way, k))
+            def _():
+                i = item(way, k)
+                y_in(i, p).wait_recv()
+                x_copy(i, p, x).start()
+
+    for k in range(steps):
+        @pl.loop(0, PIECES)
+        def _(p):
+            for way in range(2):
+                @pl.when(receives(way, k))
+                def _():
+                    z_in(way, k, p).wait_recv()
+                    if k < last:
+                        @pl.when(sends(way, k + 1))
+                        def _():
+                            z_out(way, k + 1, p).start()
+                    y_out(item(way, k), p).start()
+                    if k == last:
+                        x_copy(extra(way), p, x).start()
+            if k == 0:
+                y_in(0, p).wait_recv()
+                x_copy(0, p, x).start()
+
+            @pl.when(p > 0)
+            def _():
+                pass_on(k, p - 1)
+
+            if k > 0:
+                @pl.when(p == 0)
+                def _():
+                    pass_on(k - 1, PIECES - 1)
+
+    pass_on(last, PIECES - 1)
+    own.wait()
+
+    @pl.loop(0, PIECES)
+    def _(p):
+        x_copy(0, p, 1 - x).wait_recv()
+        x_copy(0, p, x).wait_send()
+        y_out(0, p).wait_send()
+        for way in range(2):
+            for k in range(steps):
+                @pl.when(sends(way, k))
+                def _():
+                    z_out(way, k, p).wait_send()
+
+                @pl.when(receives(way, k))
+                def _():
+                    i = item(way, k)
+                    x_copy(i, p, 1 - x).wait_recv()
+                    x_copy(i, p, x).wait_send()
+                    y_out(i, p).wait_send()
+                    if k == last:
+                        x_copy(extra(way), p, 1 - x).wait_recv()
+                        x_copy(extra(way), p, x).wait_send()
+
+
+def gather(merged, count):
+    rows, wide = merged.shape
+    outer = count // 2
+    items = 2 * (outer - 1) + 1
+    dma = pltpu.SemaphoreType.DMA
+    hbm = pl.BlockSpec(memory_space=pl.ANY)
+    return pl.pallas_call(
+        functools.partial(gather_kernel, outer),
+        out_shape=jax.ShapeDtypeStruct((rows * count, wide), merged.dtype),
+        in_specs=[hbm],
+        out_specs=hbm,
+        scratch_shapes=[
+            dma((2, outer - 1, PIECES)),
+            dma((2, outer - 1, PIECES)),
+            dma((items, PIECES)),
+            dma((items, PIECES)),
+            dma((items + 2, PIECES)),
+            dma((items + 2, PIECES)),
+            dma,
+        ],
+        compiler_params=pltpu.CompilerParams(collective_id=2, has_side_effects=True),
+        cost_estimate=pl.CostEstimate(flops=0, bytes_accessed=300 << 20, transcendentals=0),
+    )(merged)
+
+
 def body(tokens, weight, adapter_a, adapter_b, short_filter, long_filter, skip_gain, cotangent):
     row_count = tokens.shape[0]
     share_rows = weight.shape[0]
@@ -332,7 +523,8 @@
     features = tokens.shape[1]
     adapter_rank = adapter_a.shape[1]
     halo = long_filter.shape[0] + BLOCK
-    seq_total = row_count * lax.axis_size("ctx")
+    count = lax.axis_size("ctx")
+    seq_total = row_count * count
     first_row = lax.axis_index("ctx") * share_rows
     before = shifted(tokens[row_count - halo :], "ctx", 1)
     after = shifted(tokens[:halo], "ctx", -1)
@@ -345,7 +537,10 @@
     merged = (
         weight.reshape(share_rows, 3 * channels).astype(jnp.float32) + adapter_scale * delta_w
     ).astype(jnp.bfloat16)
-    whole = lax.all_gather(merged, "ctx", axis=0, tiled=True)
+    if count == 8 and lax.axis_size("groups") == 2:
+        whole = gather(merged, count)
+    else:
+        whole = lax.all_gather(merged, "ctx", axis=0, tiled=True)
     packed = jnp.dot(tokens_ext, whole, preferred_element_type=jnp.float32).astype(jnp.bfloat16)
     mixed, grad_packed = mixer(
         packed, cot_ext, short_filter, long_filter, skip_gain, row_count, halo
@@ -358,7 +553,6 @@
         flat_b, grad_packed, (((1,), (1,)), ((), ())), preferred_element_type=jnp.float32
     ).astype(jnp.bfloat16)
     part_a = jnp.dot(through, tokens, preferred_element_type=jnp.float32)
-    count = lax.axis_size("ctx")
     if features % (LANES * count) == 0 and (3 * channels) % (LANES * count) == 0:
         grad_tokens, sum_a, sum_b = finish(grad_packed, whole, part_a, part_b, count)
     else:

time: 326 us -> 251 us (0.77)
  waiting for transfers between devices: 177 us -> 0.01 us
  Pallas kernels: 81.3 us -> 195 us
  between operations: 14.2 us -> 0.87 us
    all_gather x1 -> x0, waiting for transfers between devices: 134 us -> none  [body(): whole = lax.all_gather(merged, 'ctx', axis=0, tiled=True)]
    pallas_call x0 -> x1, Pallas kernels: none -> 116 us  [gather(): pl.pallas_call(functools.partial(gather_kernel, outer), out_shape=jax.Sha...]
    ppermute x3, waiting for transfers between devices: 43.4 us -> 0.01 us  [shifted(): lax.ppermute(value, axis, [(source, source + steps) for source in range(i...]
    unnamed x19 -> x23, local copies, waits for them, and re-layouts: 7.91 us -> 4.93 us
  transfers between devices with their start and end apart: 4 -> 3, of which waited for: 2 -> 0; matrix products, arithmetic and copies ran while one was open for 1% -> 6% of each run, Pallas kernels for 0% -> 46%
where the time goes in v3:
time: 251 us; the launch traced here: 250 us
  Pallas kernels  195 us (78%)
  matrix products  26.7 us (11%)
  local copies, waits for them, and re-layouts  13.6 us (5%)
  starting transfers between devices  10 us (4%)
  other arithmetic  3.48 us (1%)
    pallas_call x1, Pallas kernels, gather(): pl.pallas_call(functools.partial(gather_kernel, outer), out_shape=jax.Sha...  116 us
    pallas_call x1, Pallas kernels, mixer(): pl.pallas_call(functools.partial(mixer_kernel, rows, halo), out_shape=(ja...  55.3 us
    pallas_call x1, Pallas kernels, finish(): pl.pallas_call(functools.partial(finish_kernel, count), out_shape=(jax.Sh...  24.1 us
    dot_general x1, matrix products, body(): jnp.dot(tokens_ext, whole, preferred_element_type=jnp.float32)  15.1 us
    ppermute x3, starting transfers between devices, shifted(): lax.ppermute(value, axis, [(source, source + steps) for source in range(i...  10 us
  transfers between devices with their start and end apart: 3, of which 0 were waited for; matrix products, arithmetic and copies ran while one was open for 6% of the time, Pallas kernels for 46%

profile of v3, /device:TPU:24, one launch (start us, length us, event | category | flops | bytes accessed | tf_op | source)
XLA Modules:
  0.0 250.0 jit_solution(4560543204077370357)
XLA Ops:
  0.6 0.0 copy-start
  0.7 1.8 slice.17
  2.5 3.3 %collective-permute-start.2 = (bf16[144,1024]{1,0:T(8,128)(2,1)}, bf16[144,1024]{1,0:T(8,128)(2,1)}, u32[]{:S(2)}, u32[]{:S(2)}) collective-permute-start(bf16[144,1024]{1,0:T(8,128)(2,1)} %slice.17), channel_id=1, source_target_pairs={{2,0},{4,2},{6,4},{8,6},{10,8},{12,10},{14,12},{3,1},{5,3},{7,5},{... | collective-permute-start | bytes 884744 | tf_op jit(solution)/shard_map/ppermute | solution.py:21
  5.8 2.4 fusion.13
  8.2 3.2 %collective-permute-start = (bf16[144,2048]{1,0:T(8,128)(2,1)}, bf16[144,2048]{1,0:T(8,128)(2,1)}, u32[]{:S(2)}, u32[]{:S(2)}) collective-permute-start(bf16[144,2048]{1,0:T(8,128)(2,1)} %get-tuple-element.16), channel_id=1, source_target_pairs={{0,2},{2,4},{4,6},{6,8},{8,10},{10,12},{12,14},{1,3},{3,5},{5,7},{... | collective-permute-start | bytes 1769480 | tf_op jit(solution)/shard_map/ppermute | solution.py:21
  11.4 3.5 %collective-permute-start.1 = (bf16[144,2048]{1,0:T(8,128)(2,1)}, bf16[144,2048]{1,0:T(8,128)(2,1)}, u32[]{:S(2)}, u32[]{:S(2)}) collective-permute-start(bf16[144,2048]{1,0:T(8,128)(2,1)} %get-tuple-element.17), channel_id=1, source_target_pairs={{2,0},{4,2},{6,4},{8,6},{10,8},{12,10},{14,12},{3,1},{5,3},{7,5},{... | collective-permute-start | bytes 1769480 | tf_op jit(solution)/shard_map/ppermute | solution.py:21
  14.9 0.7 copy.14
  15.6 0.0 copy-start.7
  15.6 0.0 copy-start.8
  15.7 0.0 copy-start.6
  15.7 2.0 bitcast_convert_fusion
  17.7 0.1 copy.17
  17.8 0.1 copy.27
  17.9 3.5 %copy.16 = f32[256,3072]{1,0:T(8,128)} copy(f32[256,3072]{0,1:T(8,128)} %bitcast_convert_fusion) | data formatting | bytes 6291456 | tf_op jit(solution)/shard_map/convert_element_type | solution.py:538
  21.5 3.7 %fusion.1.shard_ref = bf16[256,3072]{1,0:T(8,128)(2,1)} fusion(f32[256,3072]{1,0:T(8,128)} %copy.16, bf16[16,3072]{1,0:T(8,128)(2,1)S(1)} %bitcast.36, bf16[2048,16]{0,1:T(8,128)(2,1)S(1)} %copy-done, s32[]{:T(128)S(6)} %select_n.3), kind=kOutput, calls=%fused_computation.3 | convolution fusion | flops 27525120 | bytes 4825092 | tf_op jit(solution)/shard_map/dot_general | solution.py:536
  25.1 115.9 %shard_map.111.whole_ref = bf16[2048,3072]{1,0:T(8,128)(2,1)} custom-call(bf16[256,3072]{1,0:T(8,128)(2,1)} %fusion.1.shard_ref), custom_call_target="tpu_custom_call" | custom-call | bytes 314572800 | tf_op jit(solution)/shard_map/pallas_call | solution.py:500
  141.0 0.0 collective-permute-done.2
  141.1 1.4 pad_maximum_fusion.cot_ref
  142.5 0.0 copy-start.3
  142.5 0.0 collective-permute-done
  142.5 0.0 collective-permute-done.1
  142.5 15.1 %convolution_convert_fusion.packed_ref = bf16[800,3072]{1,0:T(8,128)(2,1)} fusion(bf16[2048,3072]{1,0:T(8,128)(2,1)} %shard_map.111.whole_ref, bf16[144,2048]{1,0:T(8,128)(2,1)} %collective-permute-done.1, bf16[512,2048]{1,0:T(8,128)(2,1)S(1)} %copy-done.4, bf16[144,2048]{1,0:T(8,128)(2,1)} %collective-permute-done), kind=kOutput, calls=%fused_computation | convolution fusion | flops 10078617600 | bytes 20774912 | tf_op jit(solution)/shard_map/dot_general | solution.py:544
  157.6 55.3 %shard_map.112 = (bf16[512,1024]{1,0:T(8,128)(2,1)}, bf16[512,3072]{1,0:T(8,128)(2,1)}) custom-call(bf16[800,3072]{1,0:T(8,128)(2,1)} %convolution_convert_fusion.packed_ref, bf16[656,1024]{1,0:T(8,128)(2,1)S(1)} %pad_maximum_fusion.cot_ref, f32[21,8,128]{2,1,0:T(8,128)S(1)} %reshape.38.short_ref, f32[128,8,128]{2,1,0:T(8,128)S(1)} %bitcast.32, ...), custom_call_target="tpu_custom_call" | custom-call | flops 356515840 | bytes 12582912 | tf_op jit(solution)/shard_map/pallas_call | solution.py:153
  212.9 4.5 %fusion.7 = f32[16,2048]{1,0:T(8,128)S(1)} fusion(bf16[512,2048]{1,0:T(8,128)(2,1)} %param.8, bf16[512,3072]{1,0:T(8,128)(2,1)} %get-tuple-element.9.grad_ref, bf16[16,3072]{1,0:T(8,128)(2,1)S(1)} %bitcast.37), kind=kOutput, calls=%fused_computation.13 | convolution fusion | flops 83894272 | bytes 5472256 | tf_op jit(solution)/shard_map/dot_general | solution.py:555
  217.4 3.5 %fusion.8 = f32[16,3072]{1,0:T(8,128)S(1)} fusion(bf16[512,3072]{1,0:T(8,128)(2,1)S(1)} %copy-done.1, bf16[512,2048]{1,0:T(8,128)(2,1)} %param.8, bf16[2048,16]{0,1:T(8,128)(2,1)S(1)} %copy-done), kind=kOutput, calls=%fused_computation.14 | convolution fusion | flops 83894272 | bytes 5505024 | tf_op jit(solution)/shard_map/dot_general | solution.py:549
  221.0 24.1 %shard_map.113 = (bf16[512,1024]{1,0:T(8,128)(2,1)S(1)}, f32[8,16,640]{2,1,0:T(8,128)S(1)}) custom-call(bf16[512,3072]{1,0:T(8,128)(2,1)S(1)} %copy-done.1, bf16[2048,3072]{1,0:T(8,128)(2,1)} %shard_map.111.whole_ref, f32[8,16,640]{2,1,0:T(8,128)S(1)} %maximum_bitcast_fusion.terms_ref), custom_call_target="tpu_custom_call" | custom-call | flops 6442450944 | bytes 20971520 | tf_op jit(solution)/shard_map/pallas_call | solution.py:289
  245.1 1.0 copy-done.2
  246.1 0.1 copy.21
  246.2 0.7 copy.26
  246.9 0.1 mul.40
  247.0 0.8 copy.22
  247.8 2.3 copy.33
  (19 shorter events, 0.2 us)
Async XLA Ops:
  0.6 20.8 %copy-start = (bf16[2048,16]{0,1:T(8,128)(2,1)S(1)}, bf16[2048,16]{0,1:T(8,128)(2,1)}, u32[]{:S(2)}) copy-start(bf16[2048,16]{0,1:T(8,128)(2,1)} %param.10) | copy-start | bytes 196612
  0.6 14.3 %copy-start.5 = (bf16[256,3,1024]{2,0,1:T(8,128)(2,1)S(1)}, bf16[256,3,1024]{2,0,1:T(8,128)(2,1)}, u32[]{:S(2)}) copy-start(bf16[256,3,1024]{2,0,1:T(8,128)(2,1)} %param.9) | copy-start | bytes 4718596
  2.5 138.6 %collective-permute-start.2 = (bf16[144,1024]{1,0:T(8,128)(2,1)}, bf16[144,1024]{1,0:T(8,128)(2,1)}, u32[]{:S(2)}, u32[]{:S(2)}) collective-permute-start(bf16[144,1024]{1,0:T(8,128)(2,1)} %slice.17), channel_id=1, source_target_pairs={{2,0},{4,2},{6,4},{8,6},{10,8},{12,10},{14,12},{3,1},{5,3},{7,5},{... | collective-permute-start | bytes 884744 | tf_op jit(solution)/shard_map/ppermute | solution.py:21
  8.2 134.3 %collective-permute-start = (bf16[144,2048]{1,0:T(8,128)(2,1)}, bf16[144,2048]{1,0:T(8,128)(2,1)}, u32[]{:S(2)}, u32[]{:S(2)}) collective-permute-start(bf16[144,2048]{1,0:T(8,128)(2,1)} %get-tuple-element.16), channel_id=1, source_target_pairs={{0,2},{2,4},{4,6},{6,8},{8,10},{10,12},{12,14},{1,3},{3,5},{5,7},{... | collective-permute-start | bytes 1769480 | tf_op jit(solution)/shard_map/ppermute | solution.py:21
  11.4 131.1 %collective-permute-start.1 = (bf16[144,2048]{1,0:T(8,128)(2,1)}, bf16[144,2048]{1,0:T(8,128)(2,1)}, u32[]{:S(2)}, u32[]{:S(2)}) collective-permute-start(bf16[144,2048]{1,0:T(8,128)(2,1)} %get-tuple-element.17), channel_id=1, source_target_pairs={{2,0},{4,2},{6,4},{8,6},{10,8},{12,10},{14,12},{3,1},{5,3},{7,5},{... | collective-permute-start | bytes 1769480 | tf_op jit(solution)/shard_map/ppermute | solution.py:21
  15.6 2.1 copy-start.7
  15.6 2.1 copy-start.8
  15.7 2.2 copy-start.6
  25.1 117.4 %copy-start.4 = (bf16[512,2048]{1,0:T(8,128)(2,1)S(1)}, bf16[512,2048]{1,0:T(8,128)(2,1)}, u32[]{:S(2)}) copy-start(bf16[512,2048]{1,0:T(8,128)(2,1)} %param.8) | copy-start | bytes 6291460
  142.5 15.1 %copy-start.3 = (f32[1024]{0:T(1024)S(1)}, f32[1024]{0:T(1024)}, u32[]{:S(2)}) copy-start(f32[1024]{0:T(1024)} %param.14) | copy-start | bytes 12292
  212.9 4.5 %copy-start.1 = (bf16[512,3072]{1,0:T(8,128)(2,1)S(1)}, bf16[512,3072]{1,0:T(8,128)(2,1)}, u32[]{:S(2)}) copy-start(bf16[512,3072]{1,0:T(8,128)(2,1)} %get-tuple-element.9.grad_ref) | copy-start | bytes 9437188
  245.1 1.0 copy-start.2

commit v4 on v3

--- a/solution.py
+++ b/solution.py
@@ -13,6 +13,7 @@
 SUB = 8
 BLOCK = 16
 CHUNK = 32
+GROUP = 8
 
 
 def shifted(value, axis, steps):
@@ -39,7 +40,7 @@
 
 def mixer_kernel(
     rows, halo, packed_ref, cot_ref, short_ref, long_ref, skip_ref, mixed_ref, grad_ref,
-    p0, p1, p2, cot, query, keyed, valued, gated, gradf,
+    p0, p1, p2, cot, query, keyed, valued, gated, gradf, gated_two, gradf_two,
 ):
     channels = SUB * LANES
     short_taps = short_ref.shape[0] // 3
@@ -85,7 +86,16 @@
         put(query, at, que)
         put(gradf, at, rounded(que * tiles(cot, at, SUB)))
 
-    zero = tuple(jnp.zeros((SUB, LANES), jnp.float32) for _ in range(BLOCK))
+    apart = (rows + BLOCK) // 2
+
+    @pl.loop(0, (apart + long_taps) // SUB)
+    def _(i):
+        at = i * SUB
+        for source, target in ((gated, gated_two), (gradf, gradf_two)):
+            both = jnp.concatenate([tiles(source, at, SUB), tiles(source, at + apart, SUB)], axis=1)
+            target[pl.ds(at, SUB)] = both.astype(jnp.bfloat16)
+
+    zero = tuple(jnp.zeros((2 * SUB, LANES), jnp.float32) for _ in range(SUB))
 
     def long_sum(ref, base, sign):
         def chunk(c, acc):
@@ -97,30 +107,38 @@
 
             def at(k):
                 if k not in seen:
-                    seen[k] = ref[pl.ds(pl.multiple_of((low + k) * SUB, SUB), SUB), :]
+                    seen[k] = ref[low + k]
                 return seen[k]
 
-            for j in range(CHUNK):
-                tap = long_ref[tap0 + j]
-                for i in range(BLOCK):
-                    k = i + (CHUNK - 1) - j if sign < 0 else i + j
-                    acc[i] = acc[i] + tap * at(k)
+            for group in range(CHUNK // GROUP):
+                taps = [long_ref[tap0 + group * GROUP + j] for j in range(GROUP)]
+                for i in range(SUB):
+                    terms = []
+                    for j in range(GROUP):
+                        tap = group * GROUP + j
+                        k = i + (CHUNK - 1) - tap if sign < 0 else i + tap
+                        terms.append(taps[j] * at(k))
+                    while len(terms) > 1:
+                        terms = [terms[n] + terms[n + 1] for n in range(0, len(terms), 2)]
+                    acc[i] = acc[i] + terms[0].astype(jnp.float32)
             return tuple(acc)
 
         return lax.fori_loop(0, long_taps // CHUNK, chunk, zero)
 
-    @pl.loop(0, (rows + BLOCK) // BLOCK)
+    @pl.loop(0, apart // SUB)
     def _(b):
-        at = b * BLOCK
         skip = skip_ref[...]
-        ahead = jnp.stack(long_sum(gated, at + long_taps, -1))
-        filtered = ahead + skip[None] * tiles(gated, at + long_taps, BLOCK)
-        back = jnp.stack(long_sum(gradf, at, 1))
-        grad_gated = back + skip[None] * tiles(gradf, at, BLOCK)
-        put(p0, at, rounded(tiles(cot, at, BLOCK) * filtered))
-        put(p1, at, rounded(grad_gated * tiles(valued, at + long_taps, BLOCK)))
-        put(p2, at, rounded(grad_gated * tiles(keyed, at + long_taps, BLOCK)))
-        put(gated, at, tiles(query, at, BLOCK) * filtered)
+        ahead = jnp.stack(long_sum(gated_two, b * SUB + long_taps, -1))
+        back = jnp.stack(long_sum(gradf_two, b * SUB, 1))
+        for side in range(2):
+            at = b * SUB + side * apart
+            pick = slice(side * SUB, (side + 1) * SUB)
+            filtered = ahead[:, pick] + skip[None] * tiles(gated, at + long_taps, SUB)
+            grad_gated = back[:, pick] + skip[None] * tiles(gradf, at, SUB)
+            put(p0, at, rounded(tiles(cot, at, SUB) * filtered))
+            put(p1, at, rounded(grad_gated * tiles(valued, at + long_taps, SUB)))
+            put(p2, at, rounded(grad_gated * tiles(keyed, at + long_taps, SUB)))
+            put(cot, at, tiles(query, at, SUB) * filtered)
 
     results = (query, keyed, valued)
 
@@ -135,7 +153,7 @@
         at = pl.multiple_of(i * BLOCK, BLOCK)
         for s in range(SUB):
             pick = pl.ds(at * SUB + s, BLOCK, stride=SUB)
-            mixed_ref[pl.ds(at, BLOCK), pl.ds(s * LANES, LANES)] = gated[pick, :].astype(jnp.bfloat16)
+            mixed_ref[pl.ds(at, BLOCK), pl.ds(s * LANES, LANES)] = cot[pick, :].astype(jnp.bfloat16)
             for g in range(3):
                 grad_ref[pl.ds(at, BLOCK), pl.ds(g * channels + s * LANES, LANES)] = results[g][
                     pick, :
@@ -150,6 +168,9 @@
     scratch = [pltpu.VMEM((full, LANES), jnp.float32)] * 3 + [
         pltpu.VMEM((side, LANES), jnp.float32)
     ] * 6
+    pairs = ((rows + BLOCK) // 2 + long_taps, 2 * SUB, LANES)
+    scratch += [pltpu.VMEM(pairs, jnp.bfloat16)] * 2
+    taps = long_filter.reshape(long_taps, SUB, LANES).astype(jnp.bfloat16)
     return pl.pallas_call(
         functools.partial(mixer_kernel, rows, halo),
         out_shape=(
@@ -167,7 +188,7 @@
         packed,
         cot,
         short_filter.reshape(-1, SUB, LANES),
-        long_filter.reshape(long_taps, SUB, LANES),
+        jnp.concatenate([taps, taps], axis=1),
         skip_gain.reshape(SUB, LANES),
     )
 
@@ -326,7 +347,7 @@
 
 
 MESH = pl.DeviceIdType.MESH
-PIECES = 4
+PIECES = 8
 
 
 def gather_kernel(

time: 251 us -> 260 us (1.036)
  Pallas kernels: 195 us -> 206 us
    pallas_call x1, Pallas kernels: 55.3 us -> 60.4 us  [mixer(): pl.pallas_call(functools.partial(mixer_kernel, rows, halo), out_shape=(ja...]
    pallas_call x1, Pallas kernels: 116 us -> 120 us  [gather(): pl.pallas_call(functools.partial(gather_kernel, outer), out_shape=jax.Sha...]
    unnamed x23 -> x21, local copies, waits for them, and re-layouts: 4.93 us -> 5.21 us
  transfers between devices with their start and end apart: 3 -> 3, of which waited for: 0 -> 0; matrix products, arithmetic and copies ran while one was open for 6% -> 5% of each run, Pallas kernels for 46% -> 46%
where the time goes in v4:
time: 260 us; the launch traced here: 259 us
  Pallas kernels  206 us (79%)
  matrix products  24.8 us (10%)
  local copies, waits for them, and re-layouts  13.6 us (5%)
  starting transfers between devices  10 us (4%)
  other arithmetic  4.37 us (2%)
    pallas_call x1, Pallas kernels, gather(): pl.pallas_call(functools.partial(gather_kernel, outer), out_shape=jax.Sha...  120 us
    pallas_call x1, Pallas kernels, mixer(): pl.pallas_call(functools.partial(mixer_kernel, rows, halo), out_shape=(ja...  60.4 us
    pallas_call x1, Pallas kernels, finish(): pl.pallas_call(functools.partial(finish_kernel, count), out_shape=(jax.Sh...  25.6 us
    dot_general x1, matrix products, body(): jnp.dot(tokens_ext, whole, preferred_element_type=jnp.float32)  15.1 us
    ppermute x3, starting transfers between devices, shifted(): lax.ppermute(value, axis, [(source, source + steps) for source in range(i...  10 us
    unnamed x21, local copies, waits for them, and re-layouts  5.21 us
  transfers between devices with their start and end apart: 3, of which 0 were waited for; matrix products, arithmetic and copies ran while one was open for 5% of the time, Pallas kernels for 46%

profile of v4, /device:TPU:24, one launch (start us, length us, event | category | flops | bytes accessed | tf_op | source)
XLA Modules:
  0.0 259.3 jit_solution(2678550773139900920)
XLA Ops:
  0.6 0.0 copy-start
  0.7 1.8 slice.17
  2.5 3.3 %collective-permute-start.2 = (bf16[144,1024]{1,0:T(8,128)(2,1)}, bf16[144,1024]{1,0:T(8,128)(2,1)}, u32[]{:S(2)}, u32[]{:S(2)}) collective-permute-start(bf16[144,1024]{1,0:T(8,128)(2,1)} %slice.17), channel_id=1, source_target_pairs={{2,0},{4,2},{6,4},{8,6},{10,8},{12,10},{14,12},{3,1},{5,3},{7,5},{... | collective-permute-start | bytes 884744 | tf_op jit(solution)/shard_map/ppermute | solution.py:22
  5.8 2.4 fusion.13
  8.2 3.2 %collective-permute-start = (bf16[144,2048]{1,0:T(8,128)(2,1)}, bf16[144,2048]{1,0:T(8,128)(2,1)}, u32[]{:S(2)}, u32[]{:S(2)}) collective-permute-start(bf16[144,2048]{1,0:T(8,128)(2,1)} %get-tuple-element.16), channel_id=1, source_target_pairs={{0,2},{2,4},{4,6},{6,8},{8,10},{10,12},{12,14},{1,3},{3,5},{5,7},{... | collective-permute-start | bytes 1769480 | tf_op jit(solution)/shard_map/ppermute | solution.py:22
  11.4 3.5 %collective-permute-start.1 = (bf16[144,2048]{1,0:T(8,128)(2,1)}, bf16[144,2048]{1,0:T(8,128)(2,1)}, u32[]{:S(2)}, u32[]{:S(2)}) collective-permute-start(bf16[144,2048]{1,0:T(8,128)(2,1)} %get-tuple-element.17), channel_id=1, source_target_pairs={{2,0},{4,2},{6,4},{8,6},{10,8},{12,10},{14,12},{3,1},{5,3},{7,5},{... | collective-permute-start | bytes 1769480 | tf_op jit(solution)/shard_map/ppermute | solution.py:22
  14.9 0.9 copy.25
  15.8 0.7 copy.14
  16.5 2.0 bitcast_convert_fusion
  18.5 2.4 copy.16
  20.9 0.0 copy-start.7
  20.9 1.8 fusion.1.shard_ref
  22.7 0.1 copy.17
  22.8 1.1 convert_bitcast_fusion
  24.0 0.0 copy-start.5
  24.0 119.6 %shard_map.111.whole_ref = bf16[2048,3072]{1,0:T(8,128)(2,1)} custom-call(bf16[256,3072]{1,0:T(8,128)(2,1)} %fusion.1.shard_ref), custom_call_target="tpu_custom_call" | custom-call | bytes 314572800 | tf_op jit(solution)/shard_map/pallas_call | solution.py:521
  143.6 0.0 copy-start.4
  143.6 0.1 pad_maximum_fusion.1.long_ref
  143.7 1.2 pad_maximum_fusion.cot_ref
  144.9 0.0 copy-start.3
  144.9 0.3 copy-done.4
  145.3 15.1 %convolution_convert_fusion.packed_ref = bf16[800,3072]{1,0:T(8,128)(2,1)} fusion(bf16[2048,3072]{1,0:T(8,128)(2,1)} %shard_map.111.whole_ref, bf16[144,2048]{1,0:T(8,128)(2,1)} %collective-permute-done.1, bf16[512,2048]{1,0:T(8,128)(2,1)S(1)} %copy-done.4, bf16[144,2048]{1,0:T(8,128)(2,1)} %collective-permute-done), kind=kOutput, calls=%fused_computation | convolution fusion | flops 10078617600 | bytes 20774912 | tf_op jit(solution)/shard_map/dot_general | solution.py:565
  160.3 60.4 %shard_map.112 = (bf16[512,1024]{1,0:T(8,128)(2,1)}, bf16[512,3072]{1,0:T(8,128)(2,1)}) custom-call(bf16[800,3072]{1,0:T(8,128)(2,1)} %convolution_convert_fusion.packed_ref, bf16[656,1024]{1,0:T(8,128)(2,1)S(1)} %pad_maximum_fusion.cot_ref, f32[21,8,128]{2,1,0:T(8,128)S(1)} %reshape.37.short_ref, bf16[128,16,128]{2,1,0:T(8,128)(2,1)S(1)} %pad_maximum_fusion.1.long_ref, ...), custom_call_target="tpu_custom_call" | custom-call | flops 356515840 | bytes 12582912 | tf_op jit(solution)/shard_map/pallas_call | solution.py:174
  220.7 4.5 %fusion.7 = f32[16,2048]{1,0:T(8,128)S(1)} fusion(bf16[512,2048]{1,0:T(8,128)(2,1)} %param.8, bf16[512,3072]{1,0:T(8,128)(2,1)} %get-tuple-element.9.grad_ref, bf16[16,3072]{1,0:T(8,128)(2,1)S(1)} %bitcast.38), kind=kOutput, calls=%fused_computation.13 | convolution fusion | flops 83894272 | bytes 5472256 | tf_op jit(solution)/shard_map/dot_general | solution.py:576
  225.2 3.5 %fusion.8 = f32[16,3072]{1,0:T(8,128)S(1)} fusion(bf16[512,3072]{1,0:T(8,128)(2,1)S(1)} %copy-done.1, bf16[512,2048]{1,0:T(8,128)(2,1)} %param.8, bf16[2048,16]{0,1:T(8,128)(2,1)S(1)} %copy-done), kind=kOutput, calls=%fused_computation.14 | convolution fusion | flops 83894272 | bytes 5505024 | tf_op jit(solution)/shard_map/dot_general | solution.py:570
  228.8 25.6 %shard_map.113 = (bf16[512,1024]{1,0:T(8,128)(2,1)S(1)}, f32[8,16,640]{2,1,0:T(8,128)S(1)}) custom-call(bf16[512,3072]{1,0:T(8,128)(2,1)S(1)} %copy-done.1, bf16[2048,3072]{1,0:T(8,128)(2,1)} %shard_map.111.whole_ref, f32[8,16,640]{2,1,0:T(8,128)S(1)} %maximum_bitcast_fusion.terms_ref), custom_call_target="tpu_custom_call" | custom-call | flops 6442450944 | bytes 20971520 | tf_op jit(solution)/shard_map/pallas_call | solution.py:310
  254.4 1.0 copy-done.2
  255.4 0.1 copy.21
  255.5 0.7 copy.26
  256.2 0.1 mul.40
  256.3 0.8 copy.22
  257.1 2.3 copy.33
  (19 shorter events, 0.2 us)
Async XLA Ops:
  0.6 20.3 %copy-start = (bf16[2048,16]{0,1:T(8,128)(2,1)S(1)}, bf16[2048,16]{0,1:T(8,128)(2,1)}, u32[]{:S(2)}) copy-start(bf16[2048,16]{0,1:T(8,128)(2,1)} %param.10) | copy-start | bytes 196612
  0.6 15.2 %copy-start.6 = (bf16[256,3,1024]{2,0,1:T(8,128)(2,1)S(1)}, bf16[256,3,1024]{2,0,1:T(8,128)(2,1)}, u32[]{:S(2)}) copy-start(bf16[256,3,1024]{2,0,1:T(8,128)(2,1)} %param.9) | copy-start | bytes 4718596
  2.5 141.2 %collective-permute-start.2 = (bf16[144,1024]{1,0:T(8,128)(2,1)}, bf16[144,1024]{1,0:T(8,128)(2,1)}, u32[]{:S(2)}, u32[]{:S(2)}) collective-permute-start(bf16[144,1024]{1,0:T(8,128)(2,1)} %slice.17), channel_id=1, source_target_pairs={{2,0},{4,2},{6,4},{8,6},{10,8},{12,10},{14,12},{3,1},{5,3},{7,5},{... | collective-permute-start | bytes 884744 | tf_op jit(solution)/shard_map/ppermute | solution.py:22
  8.2 136.7 %collective-permute-start = (bf16[144,2048]{1,0:T(8,128)(2,1)}, bf16[144,2048]{1,0:T(8,128)(2,1)}, u32[]{:S(2)}, u32[]{:S(2)}) collective-permute-start(bf16[144,2048]{1,0:T(8,128)(2,1)} %get-tuple-element.16), channel_id=1, source_target_pairs={{0,2},{2,4},{4,6},{6,8},{8,10},{10,12},{12,14},{1,3},{3,5},{5,7},{... | collective-permute-start | bytes 1769480 | tf_op jit(solution)/shard_map/ppermute | solution.py:22
  11.4 133.5 %collective-permute-start.1 = (bf16[144,2048]{1,0:T(8,128)(2,1)}, bf16[144,2048]{1,0:T(8,128)(2,1)}, u32[]{:S(2)}, u32[]{:S(2)}) collective-permute-start(bf16[144,2048]{1,0:T(8,128)(2,1)} %get-tuple-element.17), channel_id=1, source_target_pairs={{2,0},{4,2},{6,4},{8,6},{10,8},{12,10},{14,12},{3,1},{5,3},{7,5},{... | collective-permute-start | bytes 1769480 | tf_op jit(solution)/shard_map/ppermute | solution.py:22
  20.9 1.8 copy-start.7
  24.0 119.7 %copy-start.5 = (bf16[512,1024]{1,0:T(8,128)(2,1)S(1)}, bf16[512,1024]{1,0:T(8,128)(2,1)}, u32[]{:S(2)}) copy-start(bf16[512,1024]{1,0:T(8,128)(2,1)} %param.15) | copy-start | bytes 3145732
  143.6 1.7 copy-start.4
  144.9 15.4 %copy-start.3 = (f32[1024]{0:T(1024)S(1)}, f32[1024]{0:T(1024)}, u32[]{:S(2)}) copy-start(f32[1024]{0:T(1024)} %param.14) | copy-start | bytes 12292
  220.7 4.5 %copy-start.1 = (bf16[512,3072]{1,0:T(8,128)(2,1)S(1)}, bf16[512,3072]{1,0:T(8,128)(2,1)}, u32[]{:S(2)}) copy-start(bf16[512,3072]{1,0:T(8,128)(2,1)} %get-tuple-element.9.grad_ref) | copy-start | bytes 9437188
  254.4 1.0 copy-start.2

commit v5 on v3

--- a/solution.py
+++ b/solution.py
@@ -330,7 +330,8 @@
 
 
 def gather_kernel(
-    outer, shard_ref, out_ref, z_send, z_recv, y_send, y_recv, x_send, x_recv, local_sem
+    outer, halo, shard_ref, tok_ref, cot_ref, zero_ref, out_ref, tok_out, cot_out,
+    z_send, z_recv, y_send, y_recv, x_send, x_recv, local_sem, h_send, h_recv, h_zero, h_own,
 ):
     me = lax.axis_index("ctx")
     x = lax.axis_index("groups")
@@ -416,7 +417,11 @@
         pl.semaphore_signal(
             barrier, inc=1, device_id=ctx_of(lax.rem(z + step, outer), y), device_id_type=MESH
         )
-    pl.semaphore_wait(barrier, 4)
+    for step in (1, 2 * outer - 1):
+        pl.semaphore_signal(
+            barrier, inc=1, device_id={"ctx": lax.rem(me + step, 2 * outer)}, device_id_type=MESH
+        )
+    pl.semaphore_wait(barrier, 6)
 
     @pl.loop(0, PIECES)
     def _(p):
@@ -430,6 +435,39 @@
         shard_ref, out_ref.at[pl.ds(pl.multiple_of(me * rows, rows), rows)], local_sem
     )
     own.start()
+
+    count, size, cols = 2 * outer, tok_ref.shape[0], cot_ref.shape[1]
+    head, tail = pl.ds(0, halo), pl.ds(size - halo, halo)
+    spots = (
+        (tok_ref.at[tail], tok_out.at[head], zero_ref, 1),
+        (tok_ref.at[head], tok_out.at[pl.ds(size + halo, halo)], zero_ref, -1),
+        (cot_ref.at[head], cot_out.at[pl.ds(size, halo)], zero_ref.at[:, pl.ds(0, cols)], -1),
+    )
+    placed = [
+        pltpu.make_async_copy(tok_ref, tok_out.at[pl.ds(halo, size)], h_own.at[0]),
+        pltpu.make_async_copy(cot_ref, cot_out.at[pl.ds(0, size)], h_own.at[1]),
+    ]
+    halos, blanks = [], []
+    for n, (src, dst, blank, step) in enumerate(spots):
+        halos.append(copy(src, dst, h_send.at[n], h_recv.at[n], {"ctx": me + step}))
+        blanks.append(pltpu.make_async_copy(blank, dst, h_zero.at[n]))
+
+    def has_target(n):
+        return me < count - 1 if spots[n][3] > 0 else me > 0
+
+    def has_source(n):
+        return me > 0 if spots[n][3] > 0 else me < count - 1
+
+    for n in range(3):
+        @pl.when(has_target(n))
+        def _():
+            halos[n].start()
+
+        @pl.when(jnp.logical_not(has_source(n)))
+        def _():
+            blanks[n].start()
+    for one in placed:
+        one.start()
 
     def pass_on(k, p):
         for way in range(2):
@@ -468,6 +506,20 @@
 
     pass_on(last, PIECES - 1)
     own.wait()
+    for one in placed:
+        one.wait()
+    for n in range(3):
+        @pl.when(has_target(n))
+        def _():
+            halos[n].wait_send()
+
+        @pl.when(has_source(n))
+        def _():
+            halos[n].wait_recv()
+
+        @pl.when(jnp.logical_not(has_source(n)))
+        def _():
+            blanks[n].wait()
 
     @pl.loop(0, PIECES)
     def _(p):
@@ -491,17 +543,21 @@
                         x_copy(extra(way), p, x).wait_send()
 
 
-def gather(merged, count):
+def gather(merged, tokens, cotangent, halo, count):
     rows, wide = merged.shape
     outer = count // 2
     items = 2 * (outer - 1) + 1
     dma = pltpu.SemaphoreType.DMA
     hbm = pl.BlockSpec(memory_space=pl.ANY)
     return pl.pallas_call(
-        functools.partial(gather_kernel, outer),
-        out_shape=jax.ShapeDtypeStruct((rows * count, wide), merged.dtype),
-        in_specs=[hbm],
-        out_specs=hbm,
+        functools.partial(gather_kernel, outer, halo),
+        out_shape=(
+            jax.ShapeDtypeStruct((rows * count, wide), merged.dtype),
+            jax.ShapeDtypeStruct((tokens.shape[0] + 2 * halo, tokens.shape[1]), tokens.dtype),
+            jax.ShapeDtypeStruct((tokens.shape[0] + halo, cotangent.shape[1]), tokens.dtype),
+        ),
+        in_specs=[hbm] * 4,
+        out_specs=(hbm,) * 3,
         scratch_shapes=[
             dma((2, outer - 1, PIECES)),
             dma((2, outer - 1, PIECES)),
@@ -510,10 +566,14 @@
             dma((items + 2, PIECES)),
             dma((items + 2, PIECES)),
             dma,
+            dma((3,)),
+            dma((3,)),
+            dma((3,)),
+            dma((2,)),
         ],
         compiler_params=pltpu.CompilerParams(collective_id=2, has_side_effects=True),
         cost_estimate=pl.CostEstimate(flops=0, bytes_accessed=300 << 20, transcendentals=0),
-    )(merged)
+    )(merged, tokens, cotangent, jnp.zeros((halo, tokens.shape[1]), tokens.dtype))
 
 
 def body(tokens, weight, adapter_a, adapter_b, short_filter, long_filter, skip_gain, cotangent):
@@ -526,11 +586,6 @@
     count = lax.axis_size("ctx")
     seq_total = row_count * count
     first_row = lax.axis_index("ctx") * share_rows
-    before = shifted(tokens[row_count - halo :], "ctx", 1)
-    after = shifted(tokens[:halo], "ctx", -1)
-    cot_after = shifted(cotangent[:halo], "ctx", -1)
-    tokens_ext = jnp.concatenate([before, tokens, after], axis=0)
-    cot_ext = jnp.concatenate([cotangent, cot_after], axis=0)
     own_rows = lax.dynamic_slice_in_dim(adapter_a, first_row, share_rows, 0)
     flat_b = adapter_b.reshape(adapter_rank, 3 * channels)
     delta_w = jnp.dot(own_rows, flat_b, preferred_element_type=jnp.float32)
@@ -538,8 +593,13 @@
         weight.reshape(share_rows, 3 * channels).astype(jnp.float32) + adapter_scale * delta_w
     ).astype(jnp.bfloat16)
     if count == 8 and lax.axis_size("groups") == 2:
-        whole = gather(merged, count)
+        whole, tokens_ext, cot_ext = gather(merged, tokens, cotangent, halo, count)
     else:
+        before = shifted(tokens[row_count - halo :], "ctx", 1)
+        after = shifted(tokens[:halo], "ctx", -1)
+        cot_after = shifted(cotangent[:halo], "ctx", -1)
+        tokens_ext = jnp.concatenate([before, tokens, after], axis=0)
+        cot_ext = jnp.concatenate([cotangent, cot_after], axis=0)
         whole = lax.all_gather(merged, "ctx", axis=0, tiled=True)
     packed = jnp.dot(tokens_ext, whole, preferred_element_type=jnp.float32).astype(jnp.bfloat16)
     mixed, grad_packed = mixer(

time: 251 us -> 302 us (1.20)
  Pallas kernels: 195 us -> 256 us
  starting transfers between devices: 10 us -> 0 us
    pallas_call x1, Pallas kernels: 116 us -> 147 us  [gather(): pl.pallas_call(functools.partial(gather_kernel, outer, halo), out_shape=(...]
    pallas_call x1, Pallas kernels: 24.1 us -> 53 us  [finish(): pl.pallas_call(functools.partial(finish_kernel, count), out_shape=(jax.Sh...]
    ppermute x3 -> x0, starting transfers between devices: 10 us -> none  [shifted(): lax.ppermute(value, axis, [(source, source + steps) for source in range(i...]
    slice x2 -> x0, local copies, waits for them, and re-layouts: 4.21 us -> none  [the longest x1 2.38 us: body(): before = shifted(tokens[row_count - halo:], 'ctx', 1)]
    unnamed x23 -> x15, local copies, waits for them, and re-layouts: 4.93 us -> 7.84 us
  transfers between devices with their start and end apart: 3 -> 0, of which waited for: 0 -> 0; matrix products, arithmetic and copies ran while one was open for 6% -> 0% of each run, Pallas kernels for 46% -> 0%
where the time goes in v5:
time: 302 us
  Pallas kernels  256 us (85%)
  matrix products  28.1 us (9%)
  local copies, waits for them, and re-layouts  15 us (5%)
    pallas_call x1, Pallas kernels, gather(): pl.pallas_call(functools.partial(gather_kernel, outer, halo), out_shape=(...  147 us
    pallas_call x1, Pallas kernels, mixer(): pl.pallas_call(functools.partial(mixer_kernel, rows, halo), out_shape=(ja...  55.3 us
    pallas_call x1, Pallas kernels, finish(): pl.pallas_call(functools.partial(finish_kernel, count), out_shape=(jax.Sh...  53 us
    dot_general x1, matrix products, body(): jnp.dot(tokens_ext, whole, preferred_element_type=jnp.float32)  15.8 us
    unnamed x15, local copies, waits for them, and re-layouts  7.84 us

profile of v5, /device:TPU:24, one launch (start us, length us, event | category | flops | bytes accessed | tf_op | source)
XLA Modules:
  0.0 301.7 jit_solution(1041110863500638790)
XLA Ops:
  0.6 0.0 copy-start
  0.7 0.9 copy.25
  1.6 1.0 copy.17
  2.6 1.1 copy.27
  3.7 1.7 copy.14
  5.5 2.0 bitcast_convert_fusion
  7.5 3.5 %copy.16 = f32[256,3072]{1,0:T(8,128)} copy(f32[256,3072]{0,1:T(8,128)} %bitcast_convert_fusion) | data formatting | bytes 6291456 | tf_op jit(solution)/shard_map/convert_element_type | solution.py:593
  11.0 0.0 copy-done
  11.0 3.7 %fusion.1.shard_ref = bf16[256,3072]{1,0:T(8,128)(2,1)} fusion(f32[256,3072]{1,0:T(8,128)} %copy.16, bf16[16,3072]{1,0:T(8,128)(2,1)S(1)} %bitcast.37, bf16[2048,16]{0,1:T(8,128)(2,1)S(1)} %copy-done, s32[]{:T(128)S(6)} %select_n.3), kind=kOutput, calls=%fused_computation.3 | convolution fusion | flops 27525120 | bytes 4825092 | tf_op jit(solution)/shard_map/dot_general | solution.py:591
  14.7 0.9 broadcast_in_dim.3.zero_ref
  15.5 147.5 %shard_map.111 = (bf16[2048,3072]{1,0:T(8,128)(2,1)}, bf16[800,2048]{1,0:T(8,128)(2,1)}, bf16[656,1024]{1,0:T(8,128)(2,1)}) custom-call(bf16[256,3072]{1,0:T(8,128)(2,1)} %fusion.1.shard_ref, bf16[512,2048]{1,0:T(8,128)(2,1)} %tok_ref.1, bf16[512,1024]{1,0:T(8,128)(2,1)} %cot_ref.1, bf16[144,2048]{1,0:T(8,128)(2,1)} %broadcast_in_dim.3.zero_ref), custom_call_target="tpu_custom_call" | custom-call | bytes 314572800 | tf_op jit(solution)/shard_map/pallas_call | solution.py:552
  163.0 0.0 copy-start.2
  163.0 0.0 copy-start.4
  163.1 15.8 %convolution_convert_fusion.packed_ref = bf16[800,3072]{1,0:T(8,128)(2,1)} fusion(bf16[800,2048]{1,0:T(8,128)(2,1)} %get-tuple-element.11, bf16[2048,3072]{1,0:T(8,128)(2,1)} %get-tuple-element.12.whole_ref), kind=kOutput, calls=%fused_computation | convolution fusion | flops 10068787200 | bytes 20774912 | tf_op jit(solution)/shard_map/dot_general | solution.py:604
  178.9 0.0 copy-done.2
  178.9 0.0 copy-done.4
  178.9 55.3 %shard_map.112 = (bf16[512,1024]{1,0:T(8,128)(2,1)}, bf16[512,3072]{1,0:T(8,128)(2,1)}) custom-call(bf16[800,3072]{1,0:T(8,128)(2,1)} %convolution_convert_fusion.packed_ref, bf16[656,1024]{1,0:T(8,128)(2,1)S(1)} %copy-done.2, f32[21,8,128]{2,1,0:T(8,128)S(1)} %reshape.38.short_ref, f32[128,8,128]{2,1,0:T(8,128)S(1)} %bitcast.33, f32[8,128]{1,0:T(8,128)S(1)} %bitcast.36), custom_call_target="tpu_custom_call" | custom-call | flops 356515840 | bytes 12582912 | tf_op jit(solution)/shard_map/pallas_call | solution.py:153
  234.2 0.0 copy-start.1
  234.2 5.1 %fusion.2 = f32[16,2048]{1,0:T(8,128)} fusion(bf16[512,2048]{1,0:T(8,128)(2,1)} %tok_ref.1, bf16[512,3072]{1,0:T(8,128)(2,1)} %get-tuple-element.15.grad_ref, bf16[16,3072]{1,0:T(8,128)(2,1)S(1)} %bitcast.38), kind=kOutput, calls=%fused_computation.7 | convolution fusion | flops 83894272 | bytes 5472256 | tf_op jit(solution)/shard_map/dot_general | solution.py:615
  239.3 0.9 copy.31
  240.2 0.0 copy-done.1
  240.2 3.5 %fusion.3 = f32[16,3072]{1,0:T(8,128)S(1)} fusion(bf16[512,3072]{1,0:T(8,128)(2,1)S(1)} %copy-done.1, bf16[512,2048]{1,0:T(8,128)(2,1)} %tok_ref.1, bf16[2048,16]{0,1:T(8,128)(2,1)S(1)} %copy-done), kind=kOutput, calls=%fused_computation.8 | convolution fusion | flops 83894272 | bytes 5505024 | tf_op jit(solution)/shard_map/dot_general | solution.py:609
  243.8 53.0 %shard_map.113 = (bf16[512,1024]{1,0:T(8,128)(2,1)S(1)}, f32[8,16,640]{2,1,0:T(8,128)S(1)}) custom-call(bf16[512,3072]{1,0:T(8,128)(2,1)S(1)} %copy-done.1, bf16[2048,3072]{1,0:T(8,128)(2,1)} %get-tuple-element.12.whole_ref, f32[8,16,640]{2,1,0:T(8,128)S(1)} %maximum_bitcast_fusion.terms_ref), custom_call_target="tpu_custom_call" | custom-call | flops 6442450944 | bytes 20971520 | tf_op jit(solution)/shard_map/pallas_call | solution.py:289
  296.8 0.0 copy-start.3
  296.8 1.0 copy-done.3
  297.8 0.1 copy.21
  297.9 0.7 copy.26
  298.6 0.1 mul.40
  298.6 0.8 copy.22
  299.4 2.3 copy.33
  (5 shorter events, 0.1 us)
Async XLA Ops:
  0.6 10.4 %copy-start = (bf16[2048,16]{0,1:T(8,128)(2,1)S(1)}, bf16[2048,16]{0,1:T(8,128)(2,1)}, u32[]{:S(2)}) copy-start(bf16[2048,16]{0,1:T(8,128)(2,1)} %param.10) | copy-start | bytes 196612
  163.0 15.8 %copy-start.2 = (bf16[656,1024]{1,0:T(8,128)(2,1)S(1)}, bf16[656,1024]{1,0:T(8,128)(2,1)}, u32[]{:S(2)}) copy-start(bf16[656,1024]{1,0:T(8,128)(2,1)} %get-tuple-element.13.cot_ref) | copy-start | bytes 4030468
  163.0 15.8 %copy-start.4 = (f32[1024]{0:T(1024)S(1)}, f32[1024]{0:T(1024)}, u32[]{:S(2)}) copy-start(f32[1024]{0:T(1024)} %param.14) | copy-start | bytes 12292
  234.2 6.1 %copy-start.1 = (bf16[512,3072]{1,0:T(8,128)(2,1)S(1)}, bf16[512,3072]{1,0:T(8,128)(2,1)}, u32[]{:S(2)}) copy-start(bf16[512,3072]{1,0:T(8,128)(2,1)} %get-tuple-element.15.grad_ref) | copy-start | bytes 9437188
  296.8 1.0 copy-start.3
